TPU v7x, 32 devices: a whole 2x2x4 slice. The times are simulated.
32 devices in a mesh: parts: 2 (over x), wall: 16 (over z, y, core).
Axes of the slice: x: 2, y: 2, z: 4, core: 2. Of those that a mesh axis runs over, the one named last changes fastest.
Arguments:
- displacement: float32 [3, 524288], P(None, ('parts', 'wall')), parts along dimension 1, may hold values from -6 to 6
- velocity: float32 [3, 524288], P(None, ('parts', 'wall')), parts along dimension 1, may hold values from -6 to 6
- send_list: int32 [32, 16, 64], P(('parts', 'wall')), parts along dimension 0, may hold values from 0 to 16383, as said below
- arrive_list: int32 [32, 16, 64], P(('parts', 'wall')), parts along dimension 0, may hold values from 0 to 16383, as said below
- recv_count: int32 [32, 16], P(('parts', 'wall')), parts along dimension 0, may hold values from 0 to 64, as said below
- horizon_blocks: int32 [4096, 27], P(('parts', 'wall')), parts along dimension 0, may hold values from 0 to 2047, as said below
- bond_intact: int32 [4096, 27, 128], P(('parts', 'wall')), parts along dimension 0, may hold values 0 or 1
- modulus: float32 [524288], P(('parts', 'wall')), parts along dimension 0, may hold values from 0.5 to 2
- bond_weight: bfloat16 [27, 128, 128], replicated, may hold values from -0.109375 to 0.109375
Outputs:
- new_displacement: float32 [3, 524288], P(None, ('parts', 'wall')), parts along dimension 1
- new_velocity: float32 [3, 524288], P(None, ('parts', 'wall')), parts along dimension 1
There are 2 independent parts, one for each index of `parts`. A program takes and returns all parts, laid end to end along the dimension named above; an argument that names none is the same for every part. Nothing has to cross between parts.
Inputs may be any that keep to these rules, and one draw needn't show every extreme that they name: For c < recv_count[d, s], send_list[s, d, c] is the local index on owner s of a node handed to owner d; the nodes that s hands away are distinct, and every owner hands away as many nodes as it receives. Other slots hold 0. For c < recv_count[d, s], arrive_list[d, s, c] is the local index on owner d where the c-th node from s lands; over all s and c these are exactly the local indices that d hands away, each once. Other slots hold 0. recv_count[d, s] is 0 for s = d and at least 1 otherwise; at most 64 nodes go from one owner to one other owner, and that many do on some pair in every draw. `horizon_blocks`: block b lies in layer b // 64; every block listed for b lies in the same layer, the layer before or the layer after.
All inputs are finite; a program needn't handle non-finite values. No bound on the sum of `bond_intact` on one device may be relied on, other than what follows from the above.
Results may differ from a plain program's by a relative error of at most 0.0011.
Values may be sent and summed in bfloat16 or wider, within the bound.
A program may use at most 64 MiB of HBM per device.

v0:
```python
import jax
import jax.numpy as jnp
from jax import lax
from jax.sharding import PartitionSpec as P

SUBSTEPS = 2
LAYER = 64


TIME_STEP = 0.25


def with_halo(x, sides, width):
    for axis, dim in sides:
        count, length = (lax.axis_size(axis), x.shape[dim])
        up = [(i, (i + 1) % count) for i in range(count - 1)]
        down = [(j, i) for i, j in up]
        last = lax.slice_in_dim(x, length - width, length, axis=dim)
        initial = lax.slice_in_dim(x, 0, width, axis=dim)
        before = lax.ppermute(last, axis, up)
        after = lax.ppermute(initial, axis, down)
        x = jnp.concatenate([before, x, after], axis=dim)
    return x


def gather_terms(extended, local_turned, intact_turned, bond_weight):
    picked = jnp.take(extended, local_turned, axis=0)
    products = jnp.einsum("jbri,jki->jbrk", picked, bond_weight, preferred_element_type=jnp.float32)
    return jnp.sum(products * intact_turned[:, :, None, :], axis=0)


def shards(
    displacement,
    velocity,
    send_list,
    arrive_list,
    recv_count,
    horizon_blocks,
    bond_intact,
    modulus,
    bond_weight,
):
    node_count = displacement.shape[1]
    block_count = horizon_blocks.shape[0]
    block_width = node_count // block_count
    capacity = send_list.shape[2]
    stacked_state = jnp.concatenate([displacement, velocity], axis=0)
    outgoing = jnp.take(stacked_state, send_list[0].reshape(-1), axis=1)
    incoming = lax.all_to_all(outgoing, "wall", split_axis=1, concat_axis=1, tiled=True)
    live_slot = jnp.arange(capacity, dtype=jnp.int32)[None, :] < recv_count[0][:, None]
    landing = jnp.where(live_slot, arrive_list[0], node_count).reshape(-1)
    stacked_state = stacked_state.at[:, landing].set(incoming, mode="drop")
    blocked_state = jnp.transpose(stacked_state.reshape(6, block_count, block_width), (1, 0, 2))
    position = blocked_state[:, :3]
    velocity_now = blocked_state[:, 3:]
    offset = lax.axis_index("wall") * block_count - LAYER
    local_turned = jnp.transpose(horizon_blocks - offset)
    intact_float = bond_intact.astype(jnp.float32)
    intact_turned = jnp.transpose(intact_float, (1, 0, 2))
    row_totals = jnp.sum(bond_weight.astype(jnp.float32), axis=2)
    stiffness = jnp.sum(intact_float * row_totals[None], axis=1)[:, None, :]
    scaling = modulus.reshape(block_count, 1, block_width)

    def force_of(current):
        rounded = lax.optimization_barrier(current.astype(jnp.bfloat16))
        widened = rounded.astype(jnp.float32)
        extended = with_halo(rounded, (("wall", 0),), LAYER)
        summed = gather_terms(extended, local_turned, intact_turned, bond_weight)
        stretch = scaling * (summed - stiffness * widened)
        dilatation = jnp.mean(stretch, axis=1, keepdims=True)
        soften = 1.0 / (1.0 + dilatation * dilatation)
        soft_low = lax.optimization_barrier(soften.astype(jnp.bfloat16))
        weighted = (soft_low.astype(jnp.float32) * widened).astype(jnp.bfloat16)
        packed = jnp.concatenate([weighted, soft_low], axis=1)
        packed_rim = with_halo(packed, (("wall", 0),), LAYER)
        paired = gather_terms(packed_rim, local_turned, intact_turned, bond_weight)
        return 0.5 * (scaling * (paired[:, :3] - widened * paired[:, 3:4]) + soften * stretch)

    acceleration = force_of(position)
    for substep in range(SUBSTEPS):
        position = position + TIME_STEP * velocity_now + 0.5 * TIME_STEP * TIME_STEP * acceleration
        following = force_of(position)
        velocity_now = velocity_now + 0.5 * TIME_STEP * (acceleration + following)
        acceleration = following
    final_position = jnp.transpose(position, (1, 0, 2)).reshape(3, node_count)
    final_speed = jnp.transpose(velocity_now, (1, 0, 2)).reshape(3, node_count)
    return (final_position, final_speed)


def solution(mesh):
    in_specs = (
        P(None, ("parts", "wall")),
        P(None, ("parts", "wall")),
        P(("parts", "wall"), None, None),
        P(("parts", "wall"), None, None),
        P(("parts", "wall"), None),
        P(("parts", "wall"), None),
        P(("parts", "wall"), None, None),
        P(("parts", "wall")),
        P(),
    )
    out_specs = (P(None, ("parts", "wall")), P(None, ("parts", "wall")))
    return jax.shard_map(shards, mesh=mesh, in_specs=in_specs, out_specs=out_specs, check_vma=False)
```

profile of v0, /device:TPU:5, one launch (start us, length us, event | category | flops | bytes accessed | tf_op | source)
XLA Modules:
  0.0 192.2 jit_solution(3010273720178321579)
XLA Ops:
  0.6 0.8 reshape_squeeze.6
  1.4 0.7 compare_and_fusion.1
  2.1 1.1 pad_maximum_fusion
  3.3 5.3 %copy.106 = f32[6,16384]{0,1:T(8,128)} copy(f32[6,16384]{1,0:T(8,128)S(1)} %pad_maximum_fusion) | data formatting | bytes 786432 | tf_op jit(solution)/shard_map/concatenate | solution.py:47
  8.6 6.3 %gather_fusion = f32[1024,6]{1,0:T(8,128)S(1)} fusion(f32[6,16384]{0,1:T(8,128)} %copy.106, s32[1024]{0:T(1024)S(1)} %broadcast_clamp_fusion), kind=kCustom, calls=%fused_computation.6 | custom fusion | bytes 53248 | tf_op jit(solution)/shard_map/jit(_take)/gather | solution.py:48
  15.8 6.6 %all-to-all-start = ((f32[16,1,384]{2,1,0:T(1,128)}), f32[16,1,384]{2,1,0:T(1,128)S(1)}, u32[]{:S(2)}, u32[]{:S(2)}) async-start(f32[16,1,384]{2,1,0:T(1,128)} %reshape.321), calls=%async_computation | async-start | bytes 49152 | tf_op jit(solution)/shard_map/all_to_all | solution.py:49
  22.8 1.4 convert_bitcast_fusion
  24.7 2.8 %all-to-all-done = f32[16,1,384]{2,1,0:T(1,128)S(1)} async-done(((f32[16,1,384]{2,1,0:T(1,128)}), f32[16,1,384]{2,1,0:T(1,128)S(1)}, u32[]{:S(2)}, u32[]{:S(2)}) %all-to-all-start) | async-done | bytes 24608 | tf_op jit(solution)/shard_map/all_to_all | solution.py:49
  29.1 9.6 %scatter_fusion = f32[6,16384]{0,1:T(8,128)} fusion(f32[6,16384]{0,1:T(8,128)} %copy.106, s32[1024]{0:T(1024)S(1)} %bitcast.102, f32[1024,6]{1,0:T(8,128)S(1)} %copy.107), kind=kCustom, calls=%fused_computation.7 | custom fusion | bytes 77824 | tf_op jit(solution)/shard_map/scatter | solution.py:52
  38.8 5.5 %copy.108 = f32[6,128,128]{2,0,1:T(8,128)S(1)} copy(f32[6,128,128]{0,2,1:T(8,128)} %bitcast.81) | data formatting | bytes 786432 | tf_op jit(solution)/shard_map/reshape | solution.py:53
  44.4 3.4 %collective-permute-start = (bf16[64,3,128]{2,1,0:T(4,128)(2,1)S(1)}, bf16[64,3,128]{2,1,0:T(4,128)(2,1)S(1)}, u32[]{:S(2)}, u32[]{:S(2)}) collective-permute-start(bf16[64,3,128]{2,1,0:T(4,128)(2,1)S(1)} %get-tuple-element.24), channel_id=1, source_target_pairs={{0,1},{1,2},{2,3},{3,4},{4,5},{5,6},{6,7},{7,8},{8,9},{9,10},{10,1... | collective-permute-start | bytes 147464 | tf_op jit(solution)/shard_map/ppermute | solution.py:20
  47.8 1.9 collective-permute-start.1
  49.7 4.5 %collective-permute-done.1 = bf16[64,3,128]{2,1,0:T(4,128)(2,1)S(1)} collective-permute-done((bf16[64,3,128]{2,1,0:T(4,128)(2,1)S(1)}, bf16[64,3,128]{2,1,0:T(4,128)(2,1)S(1)}, u32[]{:S(2)}, u32[]{:S(2)}) %collective-permute-start.1) | collective-permute-done | bytes 49184 | tf_op jit(solution)/shard_map/ppermute | solution.py:21
  54.4 10.6 %gather_fusion.1 = bf16[3456,3,128]{2,1,0:T(4,128)(2,1)} fusion(bf16[256,3,128]{2,1,0:T(4,128)(2,1)S(1)} %pad_maximum_fusion.1, s32[4096]{0:T(1024)S(1)} %pad_clamp_fusion), kind=kCustom, calls=%fused_computation.clone | custom fusion | bytes 5322240 | tf_op jit(solution)/shard_map/jit(_take)/gather | solution.py:27
  65.0 2.5 %copy.109 = bf16[3456,3,128]{2,0,1:T(8,128)(2,1)S(1)} copy(bf16[3456,3,128]{2,1,0:T(4,128)(2,1)} %gather_fusion.1) | data formatting | bytes 5308416 | tf_op jit(solution)/shard_map/jit(_take)/gather | solution.py:27
  67.6 1.4 multiply_reduce_fusion.5
  69.7 1.9 collective-permute-start.2
  71.7 2.4 %collective-permute-start.3 = (bf16[64,4,128]{2,1,0:T(4,128)(2,1)S(1)}, bf16[64,4,128]{2,1,0:T(4,128)(2,1)S(1)}, u32[]{:S(2)}, u32[]{:S(2)}) collective-permute-start(bf16[64,4,128]{2,1,0:T(4,128)(2,1)S(1)} %get-tuple-element.19), channel_id=1, source_target_pairs={{1,0},{2,1},{3,2},{4,3},{5,4},{6,5},{7,6},{8,7},{9,8},{10,9},{11,1... | collective-permute-start | bytes 196616 | tf_op jit(solution)/shard_map/ppermute | solution.py:21
  74.1 4.1 %collective-permute-done.3 = bf16[64,4,128]{2,1,0:T(4,128)(2,1)S(1)} collective-permute-done((bf16[64,4,128]{2,1,0:T(4,128)(2,1)S(1)}, bf16[64,4,128]{2,1,0:T(4,128)(2,1)S(1)}, u32[]{:S(2)}, u32[]{:S(2)}) %collective-permute-start.3) | collective-permute-done | bytes 65568 | tf_op jit(solution)/shard_map/ppermute | solution.py:21
  78.3 10.6 %gather_fusion.2 = bf16[3456,4,128]{2,1,0:T(4,128)(2,1)} fusion(bf16[256,4,128]{2,1,0:T(4,128)(2,1)S(1)} %pad_maximum_fusion.2, s32[4096]{0:T(1024)S(1)} %pad_clamp_fusion), kind=kCustom, calls=%fused_computation.1.clone | custom fusion | bytes 7091712 | tf_op jit(solution)/shard_map/jit(_take)/gather | solution.py:27
  88.9 2.6 %copy.113 = bf16[3456,4,128]{2,0,1:T(8,128)(2,1)S(1)} copy(bf16[3456,4,128]{2,1,0:T(4,128)(2,1)} %gather_fusion.2) | data formatting | bytes 7077888 | tf_op jit(solution)/shard_map/jit(_take)/gather | solution.py:27
  91.5 2.0 %multiply_reduce_fusion.2 = f32[128,4,128]{2,0,1:T(8,128)S(1)} fusion(f32[27,128,128]{2,1,0:T(8,128)S(1)} %copy-done.3, bf16[27,128,128]{2,1,0:T(8,128)(2,1)S(1)} %copy-done.8, bf16[27,128,4,128]{3,1,0,2:T(8,128)(2,1)S(1)} %bitcast.87, pred[27,128]{1,0:T(8,128)(4,1)S(1)} %compare_and_fusion), kind=kOutput, calls=%fused_computation.10 | convolution fusion | flops 458227712 | bytes 6458752 | tf_op jit(solution)/shard_map/jbri,jki->jbrk/dot_general | solution.py:28
  94.0 1.9 collective-permute-start.4
  96.0 2.6 %collective-permute-start.5 = (bf16[64,3,128]{2,1,0:T(4,128)(2,1)S(1)}, bf16[64,3,128]{2,1,0:T(4,128)(2,1)S(1)}, u32[]{:S(2)}, u32[]{:S(2)}) collective-permute-start(bf16[64,3,128]{2,1,0:T(4,128)(2,1)S(1)} %get-tuple-element.23), channel_id=1, source_target_pairs={{1,0},{2,1},{3,2},{4,3},{5,4},{6,5},{7,6},{8,7},{9,8},{10,9},{11,1... | collective-permute-start | bytes 147464 | tf_op jit(solution)/shard_map/ppermute | solution.py:21
  98.6 3.9 %collective-permute-done.5 = bf16[64,3,128]{2,1,0:T(4,128)(2,1)S(1)} collective-permute-done((bf16[64,3,128]{2,1,0:T(4,128)(2,1)S(1)}, bf16[64,3,128]{2,1,0:T(4,128)(2,1)S(1)}, u32[]{:S(2)}, u32[]{:S(2)}) %collective-permute-start.5) | collective-permute-done | bytes 49184 | tf_op jit(solution)/shard_map/ppermute | solution.py:21
  102.6 10.6 %gather_fusion.3 = bf16[3456,3,128]{2,1,0:T(4,128)(2,1)} fusion(bf16[256,3,128]{2,1,0:T(4,128)(2,1)S(1)} %pad_maximum_fusion.3, s32[4096]{0:T(1024)S(1)} %pad_clamp_fusion), kind=kCustom, calls=%fused_computation.2.clone | custom fusion | bytes 5322240 | tf_op jit(solution)/shard_map/jit(_take)/gather | solution.py:27
  113.2 2.5 %copy.116 = bf16[3456,3,128]{2,0,1:T(8,128)(2,1)S(1)} copy(bf16[3456,3,128]{2,1,0:T(4,128)(2,1)} %gather_fusion.3) | data formatting | bytes 5308416 | tf_op jit(solution)/shard_map/jit(_take)/gather | solution.py:27
  115.8 1.4 multiply_reduce_fusion.4
  117.9 1.9 collective-permute-start.6
  119.8 2.4 %collective-permute-start.7 = (bf16[64,4,128]{2,1,0:T(4,128)(2,1)S(1)}, bf16[64,4,128]{2,1,0:T(4,128)(2,1)S(1)}, u32[]{:S(2)}, u32[]{:S(2)}) collective-permute-start(bf16[64,4,128]{2,1,0:T(4,128)(2,1)S(1)} %get-tuple-element.17), channel_id=1, source_target_pairs={{1,0},{2,1},{3,2},{4,3},{5,4},{6,5},{7,6},{8,7},{9,8},{10,9},{11,1... | collective-permute-start | bytes 196616 | tf_op jit(solution)/shard_map/ppermute | solution.py:21
  122.3 4.1 %collective-permute-done.7 = bf16[64,4,128]{2,1,0:T(4,128)(2,1)S(1)} collective-permute-done((bf16[64,4,128]{2,1,0:T(4,128)(2,1)S(1)}, bf16[64,4,128]{2,1,0:T(4,128)(2,1)S(1)}, u32[]{:S(2)}, u32[]{:S(2)}) %collective-permute-start.7) | collective-permute-done | bytes 65568 | tf_op jit(solution)/shard_map/ppermute | solution.py:21
  126.5 10.6 %gather_fusion.4 = bf16[3456,4,128]{2,1,0:T(4,128)(2,1)} fusion(bf16[256,4,128]{2,1,0:T(4,128)(2,1)S(1)} %pad_maximum_fusion.4, s32[4096]{0:T(1024)S(1)} %pad_clamp_fusion), kind=kCustom, calls=%fused_computation.4.clone | custom fusion | bytes 7091712 | tf_op jit(solution)/shard_map/jit(_take)/gather | solution.py:27
  137.1 2.6 %copy.120 = bf16[3456,4,128]{2,0,1:T(8,128)(2,1)S(1)} copy(bf16[3456,4,128]{2,1,0:T(4,128)(2,1)} %gather_fusion.4) | data formatting | bytes 7077888 | tf_op jit(solution)/shard_map/jit(_take)/gather | solution.py:27
  139.7 2.0 %multiply_reduce_fusion.1 = f32[128,4,128]{2,0,1:T(8,128)S(1)} fusion(f32[27,128,128]{2,1,0:T(8,128)S(1)} %copy-done.5, bf16[27,128,128]{2,1,0:T(8,128)(2,1)S(1)} %copy-done.8, bf16[27,128,4,128]{3,1,0,2:T(8,128)(2,1)S(1)} %bitcast.88, pred[27,128]{1,0:T(8,128)(4,1)S(1)} %compare_and_fusion), kind=kOutput, calls=%fused_computation.9 | convolution fusion | flops 458227712 | bytes 6458752 | tf_op jit(solution)/shard_map/jbri,jki->jbrk/dot_general | solution.py:28
  141.7 1.2 fusion.61
  143.0 1.9 collective-permute-start.8
  144.9 2.4 %collective-permute-start.9 = (bf16[64,3,128]{2,1,0:T(4,128)(2,1)S(1)}, bf16[64,3,128]{2,1,0:T(4,128)(2,1)S(1)}, u32[]{:S(2)}, u32[]{:S(2)}) collective-permute-start(bf16[64,3,128]{2,1,0:T(4,128)(2,1)S(1)} %get-tuple-element.21), channel_id=1, source_target_pairs={{1,0},{2,1},{3,2},{4,3},{5,4},{6,5},{7,6},{8,7},{9,8},{10,9},{11,1... | collective-permute-start | bytes 147464 | tf_op jit(solution)/shard_map/ppermute | solution.py:21
  147.4 4.1 %collective-permute-done.9 = bf16[64,3,128]{2,1,0:T(4,128)(2,1)S(1)} collective-permute-done((bf16[64,3,128]{2,1,0:T(4,128)(2,1)S(1)}, bf16[64,3,128]{2,1,0:T(4,128)(2,1)S(1)}, u32[]{:S(2)}, u32[]{:S(2)}) %collective-permute-start.9) | collective-permute-done | bytes 49184 | tf_op jit(solution)/shard_map/ppermute | solution.py:21
  151.6 10.6 %gather_fusion.5 = bf16[3456,3,128]{2,1,0:T(4,128)(2,1)} fusion(bf16[256,3,128]{2,1,0:T(4,128)(2,1)S(1)} %pad_maximum_fusion.5, s32[4096]{0:T(1024)S(1)} %pad_clamp_fusion), kind=kCustom, calls=%fused_computation.3.clone | custom fusion | bytes 5322240 | tf_op jit(solution)/shard_map/jit(_take)/gather | solution.py:27
  162.2 2.5 %copy.123 = bf16[3456,3,128]{2,0,1:T(8,128)(2,1)S(1)} copy(bf16[3456,3,128]{2,1,0:T(4,128)(2,1)} %gather_fusion.5) | data formatting | bytes 5308416 | tf_op jit(solution)/shard_map/jit(_take)/gather | solution.py:27
  164.7 1.4 multiply_reduce_fusion.3
  166.9 1.9 collective-permute-start.10
  168.8 2.4 %collective-permute-start.11 = (bf16[64,4,128]{2,1,0:T(4,128)(2,1)S(1)}, bf16[64,4,128]{2,1,0:T(4,128)(2,1)S(1)}, u32[]{:S(2)}, u32[]{:S(2)}) collective-permute-start(bf16[64,4,128]{2,1,0:T(4,128)(2,1)S(1)} %get-tuple-element.15), channel_id=1, source_target_pairs={{1,0},{2,1},{3,2},{4,3},{5,4},{6,5},{7,6},{8,7},{9,8},{10,9},{11,1... | collective-permute-start | bytes 196616 | tf_op jit(solution)/shard_map/ppermute | solution.py:21
  171.2 4.1 %collective-permute-done.11 = bf16[64,4,128]{2,1,0:T(4,128)(2,1)S(1)} collective-permute-done((bf16[64,4,128]{2,1,0:T(4,128)(2,1)S(1)}, bf16[64,4,128]{2,1,0:T(4,128)(2,1)S(1)}, u32[]{:S(2)}, u32[]{:S(2)}) %collective-permute-start.11) | collective-permute-done | bytes 65568 | tf_op jit(solution)/shard_map/ppermute | solution.py:21
  175.5 10.6 %gather_fusion.6 = bf16[3456,4,128]{2,1,0:T(4,128)(2,1)} fusion(bf16[256,4,128]{2,1,0:T(4,128)(2,1)S(1)} %pad_maximum_fusion.6, s32[4096]{0:T(1024)S(1)} %pad_clamp_fusion), kind=kCustom, calls=%fused_computation.5.clone | custom fusion | bytes 7091712 | tf_op jit(solution)/shard_map/jit(_take)/gather | solution.py:27
  186.1 2.6 %copy.127 = bf16[3456,4,128]{2,0,1:T(8,128)(2,1)S(1)} copy(bf16[3456,4,128]{2,1,0:T(4,128)(2,1)} %gather_fusion.6) | data formatting | bytes 7077888 | tf_op jit(solution)/shard_map/jit(_take)/gather | solution.py:27
  188.7 2.0 %multiply_reduce_fusion = f32[128,4,128]{2,0,1:T(8,128)S(1)} fusion(f32[27,128,128]{2,1,0:T(8,128)S(1)} %copy-done.7, bf16[27,128,128]{2,1,0:T(8,128)(2,1)S(1)} %copy-done.8, bf16[27,128,4,128]{3,1,0,2:T(8,128)(2,1)S(1)} %bitcast.86, pred[27,128]{1,0:T(8,128)(4,1)S(1)} %compare_and_fusion), kind=kOutput, calls=%fused_computation.8 | convolution fusion | flops 458227712 | bytes 6458752 | tf_op jit(solution)/shard_map/jbri,jki->jbrk/dot_general | solution.py:28
  190.7 1.5 fusion.52
  (85 shorter events, 7.3 us)
Async XLA Ops:
  3.2 19.2 %copy-start.9 = (s32[128,27]{0,1:T(8,128)S(1)}, s32[128,27]{0,1:T(8,128)}, u32[]{:S(2)}) copy-start(s32[128,27]{0,1:T(8,128)} %param.18) | copy-start | bytes 41476
  3.3 19.3 %copy-start.11 = (s32[1,16]{1,0:T(1,128)S(1)}, s32[1,16]{1,0:T(1,128)}, u32[]{:S(2)}) copy-start(s32[1,16]{1,0:T(1,128)} %param.17) | copy-start | bytes 196
  3.3 19.4 %copy-start.10 = (s32[1,16,64]{2,1,0:T(8,128)S(1)}, s32[1,16,64]{2,1,0:T(8,128)}, u32[]{:S(2)}) copy-start(s32[1,16,64]{2,1,0:T(8,128)} %param.16) | copy-start | bytes 12292
  3.3 19.5 %copy-start = (s32[128,27,128]{2,0,1:T(8,128)S(1)}, s32[128,27,128]{2,0,1:T(8,128)}, u32[]{:S(2)}) copy-start(s32[128,27,128]{2,0,1:T(8,128)} %param.19) | copy-start | bytes 5308420
  8.6 15.6 %copy-start.8 = (bf16[27,128,128]{2,1,0:T(8,128)(2,1)S(1)}, bf16[27,128,128]{2,1,0:T(8,128)(2,1)}, u32[]{:S(2)}) copy-start(bf16[27,128,128]{2,1,0:T(8,128)(2,1)} %param.21) | copy-start | bytes 2654212
  15.8 11.7 %all-to-all-start = ((f32[16,1,384]{2,1,0:T(1,128)}), f32[16,1,384]{2,1,0:T(1,128)S(1)}, u32[]{:S(2)}, u32[]{:S(2)}) async-start(f32[16,1,384]{2,1,0:T(1,128)} %reshape.321), calls=%async_computation | async-start | bytes 49152 | tf_op jit(solution)/shard_map/all_to_all | solution.py:49
  44.4 5.3 %collective-permute-start = (bf16[64,3,128]{2,1,0:T(4,128)(2,1)S(1)}, bf16[64,3,128]{2,1,0:T(4,128)(2,1)S(1)}, u32[]{:S(2)}, u32[]{:S(2)}) collective-permute-start(bf16[64,3,128]{2,1,0:T(4,128)(2,1)S(1)} %get-tuple-element.24), channel_id=1, source_target_pairs={{0,1},{1,2},{2,3},{3,4},{4,5},{5,6},{6,7},{7,8},{8,9},{9,10},{10,1... | collective-permute-start | bytes 147464 | tf_op jit(solution)/shard_map/ppermute | solution.py:20
  47.8 6.5 %collective-permute-start.1 = (bf16[64,3,128]{2,1,0:T(4,128)(2,1)S(1)}, bf16[64,3,128]{2,1,0:T(4,128)(2,1)S(1)}, u32[]{:S(2)}, u32[]{:S(2)}) collective-permute-start(bf16[64,3,128]{2,1,0:T(4,128)(2,1)S(1)} %get-tuple-element.25), channel_id=1, source_target_pairs={{1,0},{2,1},{3,2},{4,3},{5,4},{6,5},{7,6},{8,7},{9,8},{10,9},{11,1... | collective-permute-start | bytes 147464 | tf_op jit(solution)/shard_map/ppermute | solution.py:21
  65.0 2.5 %copy-start.2 = (f32[27,128,128]{2,1,0:T(8,128)S(1)}, f32[27,128,128]{2,1,0:T(8,128)}, u32[]{:S(2)}) copy-start(f32[27,128,128]{2,1,0:T(8,128)} %convert_bitcast_fusion) | copy-start | bytes 5308420
  67.6 1.5 copy-start.1
  69.7 4.3 %collective-permute-start.2 = (bf16[64,4,128]{2,1,0:T(4,128)(2,1)S(1)}, bf16[64,4,128]{2,1,0:T(4,128)(2,1)S(1)}, u32[]{:S(2)}, u32[]{:S(2)}) collective-permute-start(bf16[64,4,128]{2,1,0:T(4,128)(2,1)S(1)} %get-tuple-element.18), channel_id=1, source_target_pairs={{0,1},{1,2},{2,3},{3,4},{4,5},{5,6},{6,7},{7,8},{8,9},{9,10},{10,1... | collective-permute-start | bytes 196616 | tf_op jit(solution)/shard_map/ppermute | solution.py:20
  71.7 6.5 %collective-permute-start.3 = (bf16[64,4,128]{2,1,0:T(4,128)(2,1)S(1)}, bf16[64,4,128]{2,1,0:T(4,128)(2,1)S(1)}, u32[]{:S(2)}, u32[]{:S(2)}) collective-permute-start(bf16[64,4,128]{2,1,0:T(4,128)(2,1)S(1)} %get-tuple-element.19), channel_id=1, source_target_pairs={{1,0},{2,1},{3,2},{4,3},{5,4},{6,5},{7,6},{8,7},{9,8},{10,9},{11,1... | collective-permute-start | bytes 196616 | tf_op jit(solution)/shard_map/ppermute | solution.py:21
  88.9 2.6 %copy-start.3 = (f32[27,128,128]{2,1,0:T(8,128)S(1)}, f32[27,128,128]{2,1,0:T(8,128)}, u32[]{:S(2)}) copy-start(f32[27,128,128]{2,1,0:T(8,128)} %convert_bitcast_fusion) | copy-start | bytes 5308420
  94.0 4.5 %collective-permute-start.4 = (bf16[64,3,128]{2,1,0:T(4,128)(2,1)S(1)}, bf16[64,3,128]{2,1,0:T(4,128)(2,1)S(1)}, u32[]{:S(2)}, u32[]{:S(2)}) collective-permute-start(bf16[64,3,128]{2,1,0:T(4,128)(2,1)S(1)} %get-tuple-element.22), channel_id=1, source_target_pairs={{0,1},{1,2},{2,3},{3,4},{4,5},{5,6},{6,7},{7,8},{8,9},{9,10},{10,1... | collective-permute-start | bytes 147464 | tf_op jit(solution)/shard_map/ppermute | solution.py:20
  96.0 6.5 %collective-permute-start.5 = (bf16[64,3,128]{2,1,0:T(4,128)(2,1)S(1)}, bf16[64,3,128]{2,1,0:T(4,128)(2,1)S(1)}, u32[]{:S(2)}, u32[]{:S(2)}) collective-permute-start(bf16[64,3,128]{2,1,0:T(4,128)(2,1)S(1)} %get-tuple-element.23), channel_id=1, source_target_pairs={{1,0},{2,1},{3,2},{4,3},{5,4},{6,5},{7,6},{8,7},{9,8},{10,9},{11,1... | collective-permute-start | bytes 147464 | tf_op jit(solution)/shard_map/ppermute | solution.py:21
  113.2 2.5 %copy-start.4 = (f32[27,128,128]{2,1,0:T(8,128)S(1)}, f32[27,128,128]{2,1,0:T(8,128)}, u32[]{:S(2)}) copy-start(f32[27,128,128]{2,1,0:T(8,128)} %convert_bitcast_fusion) | copy-start | bytes 5308420
  117.9 4.3 %collective-permute-start.6 = (bf16[64,4,128]{2,1,0:T(4,128)(2,1)S(1)}, bf16[64,4,128]{2,1,0:T(4,128)(2,1)S(1)}, u32[]{:S(2)}, u32[]{:S(2)}) collective-permute-start(bf16[64,4,128]{2,1,0:T(4,128)(2,1)S(1)} %get-tuple-element.16), channel_id=1, source_target_pairs={{0,1},{1,2},{2,3},{3,4},{4,5},{5,6},{6,7},{7,8},{8,9},{9,10},{10,1... | collective-permute-start | bytes 196616 | tf_op jit(solution)/shard_map/ppermute | solution.py:20
  119.8 6.5 %collective-permute-start.7 = (bf16[64,4,128]{2,1,0:T(4,128)(2,1)S(1)}, bf16[64,4,128]{2,1,0:T(4,128)(2,1)S(1)}, u32[]{:S(2)}, u32[]{:S(2)}) collective-permute-start(bf16[64,4,128]{2,1,0:T(4,128)(2,1)S(1)} %get-tuple-element.17), channel_id=1, source_target_pairs={{1,0},{2,1},{3,2},{4,3},{5,4},{6,5},{7,6},{8,7},{9,8},{10,9},{11,1... | collective-permute-start | bytes 196616 | tf_op jit(solution)/shard_map/ppermute | solution.py:21
  137.1 2.6 %copy-start.5 = (f32[27,128,128]{2,1,0:T(8,128)S(1)}, f32[27,128,128]{2,1,0:T(8,128)}, u32[]{:S(2)}) copy-start(f32[27,128,128]{2,1,0:T(8,128)} %convert_bitcast_fusion) | copy-start | bytes 5308420
  143.0 4.3 %collective-permute-start.8 = (bf16[64,3,128]{2,1,0:T(4,128)(2,1)S(1)}, bf16[64,3,128]{2,1,0:T(4,128)(2,1)S(1)}, u32[]{:S(2)}, u32[]{:S(2)}) collective-permute-start(bf16[64,3,128]{2,1,0:T(4,128)(2,1)S(1)} %get-tuple-element.20), channel_id=1, source_target_pairs={{0,1},{1,2},{2,3},{3,4},{4,5},{5,6},{6,7},{7,8},{8,9},{9,10},{10,1... | collective-permute-start | bytes 147464 | tf_op jit(solution)/shard_map/ppermute | solution.py:20
  144.9 6.5 %collective-permute-start.9 = (bf16[64,3,128]{2,1,0:T(4,128)(2,1)S(1)}, bf16[64,3,128]{2,1,0:T(4,128)(2,1)S(1)}, u32[]{:S(2)}, u32[]{:S(2)}) collective-permute-start(bf16[64,3,128]{2,1,0:T(4,128)(2,1)S(1)} %get-tuple-element.21), channel_id=1, source_target_pairs={{1,0},{2,1},{3,2},{4,3},{5,4},{6,5},{7,6},{8,7},{9,8},{10,9},{11,1... | collective-permute-start | bytes 147464 | tf_op jit(solution)/shard_map/ppermute | solution.py:21
  162.2 2.5 %copy-start.6 = (f32[27,128,128]{2,1,0:T(8,128)S(1)}, f32[27,128,128]{2,1,0:T(8,128)}, u32[]{:S(2)}) copy-start(f32[27,128,128]{2,1,0:T(8,128)} %convert_bitcast_fusion) | copy-start | bytes 5308420
  166.9 4.3 %collective-permute-start.10 = (bf16[64,4,128]{2,1,0:T(4,128)(2,1)S(1)}, bf16[64,4,128]{2,1,0:T(4,128)(2,1)S(1)}, u32[]{:S(2)}, u32[]{:S(2)}) collective-permute-start(bf16[64,4,128]{2,1,0:T(4,128)(2,1)S(1)} %get-tuple-element.14), channel_id=1, source_target_pairs={{0,1},{1,2},{2,3},{3,4},{4,5},{5,6},{6,7},{7,8},{8,9},{9,10},{10,1... | collective-permute-start | bytes 196616 | tf_op jit(solution)/shard_map/ppermute | solution.py:20
  168.8 6.5 %collective-permute-start.11 = (bf16[64,4,128]{2,1,0:T(4,128)(2,1)S(1)}, bf16[64,4,128]{2,1,0:T(4,128)(2,1)S(1)}, u32[]{:S(2)}, u32[]{:S(2)}) collective-permute-start(bf16[64,4,128]{2,1,0:T(4,128)(2,1)S(1)} %get-tuple-element.15), channel_id=1, source_target_pairs={{1,0},{2,1},{3,2},{4,3},{5,4},{6,5},{7,6},{8,7},{9,8},{10,9},{11,1... | collective-permute-start | bytes 196616 | tf_op jit(solution)/shard_map/ppermute | solution.py:21
  186.1 2.6 %copy-start.7 = (f32[27,128,128]{2,1,0:T(8,128)S(1)}, f32[27,128,128]{2,1,0:T(8,128)}, u32[]{:S(2)}) copy-start(f32[27,128,128]{2,1,0:T(8,128)} %convert_bitcast_fusion) | copy-start | bytes 5308420
where the time goes:
time: 193 us; the launch traced here: 192 us
  local copies, waits for them, and re-layouts  109 us (56%)
  starting transfers between devices  33.7 us (17%)
  waiting for transfers between devices  27.5 us (14%)
  other arithmetic  10.7 us (6%)
  matrix products  10.3 us (5%)
    gather x12, local copies, waits for them, and re-layouts, gather_terms(): picked = jnp.take(extended, local_turned, axis=0)  78.8 us
    ppermute x6, waiting for transfers between devices, with_halo(): after = lax.ppermute(initial, axis, down)  24.6 us
    ppermute x6, starting transfers between devices, with_halo(): after = lax.ppermute(initial, axis, down)  14.1 us
    ppermute x6, starting transfers between devices, with_halo(): before = lax.ppermute(last, axis, up)  13 us
    dot_general x6, matrix products, gather_terms(): jnp.einsum('jbri,jki->jbrk', picked, bond_weight, preferred_element_type=...  10.3 us
    scatter x1, local copies, waits for them, and re-layouts, shards(): stacked_state = stacked_state.at[:, landing].set(incoming, mode='drop')  9.64 us
    all_to_all x1, starting transfers between devices, shards(): lax.all_to_all(outgoing, 'wall', split_axis=1, concat_axis=1, tiled=True)  6.63 us
    gather x2, local copies, waits for them, and re-layouts, shards(): outgoing = jnp.take(stacked_state, send_list[0].reshape(-1), axis=1)  6.47 us
  transfers between devices with their start and end apart: 13, of which 7 were waited for; matrix products, arithmetic and copies ran while one was open for 1% of the time, Pallas kernels for 0%

commit v1 on v0

v1 whole, which is shorter than its diff:
```python
import functools

import jax
import jax.numpy as jnp
from jax import lax
from jax.experimental import pallas as pl
from jax.experimental.pallas import tpu as pltpu
from jax.sharding import PartitionSpec as P

SUBSTEPS = 2
LAYER = 64
TIME_STEP = 0.25
MESH = pl.DeviceIdType.MESH
F32 = jnp.float32
BF16 = jnp.bfloat16


def force_kernel(
    blocks,
    width,
    nnz,
    hor_ref,
    intact_ref,
    mod_ref,
    wt_ref,
    pos_in,
    vel_in,
    pos_ref,
    vel_ref,
    onehot_ref,
    ext_ref,
    picked_ref,
    diag_ref,
    stiff_ref,
    acc_ref,
    stretch_ref,
    soften_ref,
    send_sem,
    recv_sem,
):
    me = lax.axis_index("wall")
    count = lax.axis_size("wall")
    reach = 3 * LAYER
    slots = 2 * (SUBSTEPS + 1)
    has_left = me > 0
    has_right = me < count - 1
    left = lax.rem(me + count - 1, count)
    right = lax.rem(me + 1, count)

    barrier = pltpu.get_barrier_semaphore()

    @pl.when(has_left)
    def _():
        pl.semaphore_signal(barrier, inc=1, device_id={"wall": left}, device_id_type=MESH)

    @pl.when(has_right)
    def _():
        pl.semaphore_signal(barrier, inc=1, device_id={"wall": right}, device_id_type=MESH)

    def halo_copy(slot, half, rows):
        wide = rows * width
        if half == 0:
            source = ext_ref.at[slot, pl.ds(LAYER, LAYER), pl.ds(0, wide)]
            target = ext_ref.at[slot, pl.ds(3 * LAYER, LAYER), pl.ds(0, wide)]
            device = left
        else:
            source = ext_ref.at[slot, pl.ds(2 * LAYER, LAYER), pl.ds(0, wide)]
            target = ext_ref.at[slot, pl.ds(0, LAYER), pl.ds(0, wide)]
            device = right
        return pltpu.make_async_remote_copy(
            src_ref=source,
            dst_ref=target,
            send_sem=send_sem.at[slot, half],
            recv_sem=recv_sem.at[slot, 1 - half],
            device_id={"wall": device},
            device_id_type=MESH,
        )

    def exists(half):
        return has_left if half == 0 else has_right

    def send(slot, half, rows):
        @pl.when(exists(half))
        def _():
            halo_copy(slot, half, rows).start()

    def wait_halo(slot, half, rows):
        @pl.when(exists(half))
        def _():
            halo_copy(slot, 1 - half, rows).wait_recv()

    def own(half):
        return pl.ds(half * LAYER, LAYER)

    def put(slot, half, row, value):
        ext_ref[slot, pl.ds(LAYER + half * LAYER, LAYER), pl.ds(row * width, width)] = value

    def get(slot, half, row):
        return ext_ref[slot, pl.ds(LAYER + half * LAYER, LAYER), pl.ds(row * width, width)].astype(F32)

    pos_ref[...] = pos_in[...]
    vel_ref[...] = vel_in[...]
    for half in range(2):
        for row in range(3):
            put(0, half, row, pos_in[row, own(half), :].astype(BF16))

    @pl.when(jnp.logical_not(has_left))
    def _():
        for slot in range(slots):
            ext_ref[slot, pl.ds(0, LAYER), :] = jnp.zeros((LAYER, 4 * width), BF16)

    @pl.when(jnp.logical_not(has_right))
    def _():
        for slot in range(slots):
            ext_ref[slot, pl.ds(3 * LAYER, LAYER), :] = jnp.zeros((LAYER, 4 * width), BF16)

    pl.semaphore_wait(barrier, has_left.astype(jnp.int32) + has_right.astype(jnp.int32))

    send(0, 0, 3)
    send(0, 1, 3)

    lanes = lax.broadcasted_iota(jnp.int32, (LAYER, reach), 1)
    for half in range(2):
        local = hor_ref[own(half), :] - (me * blocks - LAYER + half * LAYER)
        for j in range(nnz):
            hit = local[:, j : j + 1] == lanes
            onehot_ref[half, pl.ds(j * LAYER, LAYER), :] = jnp.where(hit, 1.0, 0.0).astype(BF16)

    stiff = jnp.zeros((blocks, width), F32)
    zero = jnp.zeros((width, width), BF16)
    ones = jnp.ones((16, width), BF16)
    for j in range(nnz):
        weight = wt_ref[j]
        diag_ref[j, pl.ds(0, width), pl.ds(0, width)] = weight
        diag_ref[j, pl.ds(width, width), pl.ds(width, width)] = weight
        diag_ref[j, pl.ds(0, width), pl.ds(width, width)] = zero
        diag_ref[j, pl.ds(width, width), pl.ds(0, width)] = zero
        totals = jnp.dot(ones, weight, preferred_element_type=F32)[0:1, :]
        stiff = stiff + intact_ref[j] * totals
    stiff_ref[...] = stiff

    group = 9 if nnz % 9 == 0 else nnz

    def contract(slot, rows, half):
        wide = rows * width
        source = ext_ref[slot, pl.ds(half * LAYER, reach), pl.ds(0, wide)]
        for start in range(0, nnz, group):
            part = pl.ds(start * LAYER, group * LAYER)
            picked_ref[part, pl.ds(0, wide)] = jnp.dot(
                onehot_ref[half, part, :], source, preferred_element_type=F32
            ).astype(BF16)
        sums = [jnp.zeros((LAYER, width), F32) for _ in range(rows)]
        for j in range(nnz):
            part = pl.ds(j * LAYER, LAYER)
            mask = intact_ref[j, own(half), :]
            weight = diag_ref[j]
            for pair in range(2):
                first = 2 * pair
                if first + 1 < rows:
                    product = jnp.dot(
                        picked_ref[part, pl.ds(first * width, 2 * width)], weight, preferred_element_type=F32
                    )
                    sums[first] = sums[first] + product[:, :width] * mask
                    sums[first + 1] = sums[first + 1] + product[:, width:] * mask
                else:
                    product = jnp.dot(
                        picked_ref[part, pl.ds(first * width, width)], wt_ref[j], preferred_element_type=F32
                    )
                    sums[first] = sums[first] + product * mask
        return sums

    def evaluation(t, carry):
        near, far = 2 * t, 2 * t + 1
        for half in (0, 1):
            wait_halo(near, half, 3)
            summed = contract(near, 3, half)
            scaling = mod_ref[own(half), :]
            stiffness = stiff_ref[own(half), :]
            rounded = [get(near, half, row) for row in range(3)]
            stretch = [scaling * (summed[row] - stiffness * rounded[row]) for row in range(3)]
            dilatation = (stretch[0] + stretch[1] + stretch[2]) / 3.0
            soften = 1.0 / (1.0 + dilatation * dilatation)
            soft_low = soften.astype(BF16)
            soft_wide = soft_low.astype(F32)
            for row in range(3):
                put(far, half, row, (soft_wide * rounded[row]).astype(BF16))
                stretch_ref[row, own(half), :] = stretch[row]
            put(far, half, 3, soft_low)
            soften_ref[own(half), :] = soften
            send(far, half, 4)
        for half in (1, 0):
            wait_halo(far, half, 4)
            paired = contract(far, 4, half)
            scaling = mod_ref[own(half), :]
            soften = soften_ref[own(half), :]
            for row in range(3):
                rounded = get(near, half, row)
                force = 0.5 * (
                    scaling * (paired[row] - rounded * paired[3]) + soften * stretch_ref[row, own(half), :]
                )

                @pl.when(t > 0)
                def _():
                    vel_ref[row, own(half), :] = vel_ref[row, own(half), :] + 0.5 * TIME_STEP * (
                        acc_ref[row, own(half), :] + force
                    )

                acc_ref[row, own(half), :] = force

            @pl.when(t < SUBSTEPS)
            def _():
                for row in range(3):
                    moved = (
                        pos_ref[row, own(half), :]
                        + TIME_STEP * vel_ref[row, own(half), :]
                        + 0.5 * TIME_STEP * TIME_STEP * acc_ref[row, own(half), :]
                    )
                    pos_ref[row, own(half), :] = moved
                    put(2 * t + 2, half, row, moved.astype(BF16))
                send(2 * t + 2, half, 3)

        return carry

    lax.fori_loop(0, SUBSTEPS + 1, evaluation, 0)

    for half in range(2):
        @pl.when(exists(half))
        def _():
            for slot in range(slots):
                halo_copy(slot, half, 3 if slot % 2 == 0 else 4).wait_send()


def forces(horizon, intact, modulus, weight_turned, position, velocity):
    nnz, blocks, width = intact.shape
    slots = 2 * (SUBSTEPS + 1)
    vmem = pl.BlockSpec(memory_space=pltpu.VMEM)
    shape = jax.ShapeDtypeStruct((3, blocks, width), F32)
    return pl.pallas_call(
        functools.partial(force_kernel, blocks, width, nnz),
        out_shape=(shape, shape),
        in_specs=[vmem] * 6,
        out_specs=(vmem, vmem),
        scratch_shapes=[
            pltpu.VMEM((2, nnz * LAYER, 3 * LAYER), BF16),
            pltpu.VMEM((slots, 4 * LAYER, 4 * width), BF16),
            pltpu.VMEM((nnz * LAYER, 4 * width), BF16),
            pltpu.VMEM((nnz, 2 * width, 2 * width), BF16),
            pltpu.VMEM((blocks, width), F32),
            pltpu.VMEM((3, blocks, width), F32),
            pltpu.VMEM((3, blocks, width), F32),
            pltpu.VMEM((blocks, width), F32),
            pltpu.SemaphoreType.DMA((slots, 2)),
            pltpu.SemaphoreType.DMA((slots, 2)),
        ],
        compiler_params=pltpu.CompilerParams(
            collective_id=0, has_side_effects=True, vmem_limit_bytes=48 * 1024 * 1024
        ),
        name="forces",
    )(horizon, intact, modulus, weight_turned, position, velocity)


def shards(
    displacement,
    velocity,
    send_list,
    arrive_list,
    recv_count,
    horizon_blocks,
    bond_intact,
    modulus,
    bond_weight,
):
    node_count = displacement.shape[1]
    block_count = horizon_blocks.shape[0]
    block_width = node_count // block_count
    capacity = send_list.shape[2]
    stacked_state = jnp.concatenate([displacement, velocity], axis=0)
    outgoing = jnp.take(stacked_state, send_list[0].reshape(-1), axis=1)
    incoming = lax.all_to_all(outgoing, "wall", split_axis=1, concat_axis=1, tiled=True)
    live_slot = jnp.arange(capacity, dtype=jnp.int32)[None, :] < recv_count[0][:, None]
    landing = jnp.where(live_slot, arrive_list[0], node_count).reshape(-1)
    stacked_state = stacked_state.at[:, landing].set(incoming, mode="drop")
    blocked = stacked_state.reshape(6, block_count, block_width)
    intact_turned = jnp.transpose(bond_intact.astype(F32), (1, 0, 2))
    final_position, final_speed = forces(
        horizon_blocks,
        intact_turned,
        modulus.reshape(block_count, block_width),
        jnp.transpose(bond_weight, (0, 2, 1)),
        blocked[:3],
        blocked[3:],
    )
    return (final_position.reshape(3, node_count), final_speed.reshape(3, node_count))


def solution(mesh):
    in_specs = (
        P(None, ("parts", "wall")),
        P(None, ("parts", "wall")),
        P(("parts", "wall"), None, None),
        P(("parts", "wall"), None, None),
        P(("parts", "wall"), None),
        P(("parts", "wall"), None),
        P(("parts", "wall"), None, None),
        P(("parts", "wall")),
        P(),
    )
    out_specs = (P(None, ("parts", "wall")), P(None, ("parts", "wall")))
    return jax.shard_map(shards, mesh=mesh, in_specs=in_specs, out_specs=out_specs, check_vma=False)
```

time: 193 us -> 96.9 us (0.50)
  local copies, waits for them, and re-layouts: 109 us -> 51.4 us
  Pallas kernels: 0 us -> 32.5 us
  starting transfers between devices: 33.7 us -> 6.63 us
  waiting for transfers between devices: 27.5 us -> 0.79 us
  matrix products: 10.3 us -> 0 us
  other arithmetic: 10.7 us -> 4.29 us
    gather x12 -> x0, local copies, waits for them, and re-layouts: 78.8 us -> none  [gather_terms(): picked = jnp.take(extended, local_turned, axis=0)]
    pallas_call x0 -> x1, Pallas kernels: none -> 32.5 us  [forces(): pl.pallas_call(functools.partial(force_kernel, blocks, width, nnz), out_s...]
    ppermute x12 -> x0, starting transfers between devices: 27.1 us -> none  [the longest x6 14.1 us: with_halo(): after = lax.ppermute(initial, axis, down)]
    ppermute x12 -> x0, waiting for transfers between devices: 24.7 us -> none  [the longest x6 24.6 us: with_halo(): after = lax.ppermute(initial, axis, down)]
    slice x7 -> x3, local copies, waits for them, and re-layouts: 0.24 us -> 23.1 us  [the longest x2 17.9 us: shards(): blocked[3:]]
    dot_general x6 -> x0, matrix products: 10.3 us -> none  [gather_terms(): jnp.einsum('jbri,jki->jbrk', picked, bond_weight, preferred_element_type=...]
    reshape x1, local copies, waits for them, and re-layouts: 5.49 us -> 1.06 us  [shards(): final_speed.reshape(3, node_count)]
    all_to_all x1, waiting for transfers between devices: 2.79 us -> 0.79 us  [shards(): lax.all_to_all(outgoing, 'wall', split_axis=1, concat_axis=1, tiled=True)]
  transfers between devices with their start and end apart: 13 -> 1, of which waited for: 7 -> 1; matrix products, arithmetic and copies ran while one was open for 1% -> 4% of each run, Pallas kernels for 0% -> 0%
where the time goes in v1:
time: 96.9 us; the launch traced here: 96.4 us
  local copies, waits for them, and re-layouts  51.4 us (53%)
  Pallas kernels  32.5 us (34%)
  starting transfers between devices  6.63 us (7%)
  other arithmetic  4.29 us (4%)
    pallas_call x1, Pallas kernels, forces(): pl.pallas_call(functools.partial(force_kernel, blocks, width, nnz), out_s...  32.5 us
    slice x2, local copies, waits for them, and re-layouts, shards(): blocked[3:]  17.9 us
    scatter x1, local copies, waits for them, and re-layouts, shards(): stacked_state = stacked_state.at[:, landing].set(incoming, mode='drop')  9.64 us
    all_to_all x1, starting transfers between devices, shards(): lax.all_to_all(outgoing, 'wall', split_axis=1, concat_axis=1, tiled=True)  6.63 us
    gather x2, local copies, waits for them, and re-layouts, shards(): outgoing = jnp.take(stacked_state, send_list[0].reshape(-1), axis=1)  6.4 us
    concatenate x1, local copies, waits for them, and re-layouts, shards(): stacked_state = jnp.concatenate([displacement, velocity], axis=0)  5.29 us
    slice x1, local copies, waits for them, and re-layouts, shards(): blocked[:3]  5.25 us
    unnamed x14, local copies, waits for them, and re-layouts  2.79 us
  transfers between devices with their start and end apart: 1, of which 1 were waited for; matrix products, arithmetic and copies ran while one was open for 4% of the time, Pallas kernels for 0%

profile of v1, /device:TPU:5, one launch (start us, length us, event | category | flops | bytes accessed | tf_op | source)
XLA Modules:
  0.0 96.4 jit_solution(3691449183699970295)
XLA Ops:
  0.6 0.0 copy-start.4
  0.6 0.0 copy-start.3
  0.7 0.0 copy-start.1
  0.7 0.0 copy-start.2
  0.7 0.9 reshape_squeeze.6
  1.6 0.7 compare_and_fusion
  2.3 1.1 %pad_maximum_fusion = f32[6,16384]{1,0:T(8,128)S(1)} fusion(f32[3,16384]{1,0:T(4,128)} %param.10, f32[3,16384]{1,0:T(4,128)} %param.9), kind=kLoop, calls=%fused_computation.3 | loop fusion | flops 98304 | bytes 786432 | tf_op jit(solution)/shard_map/concatenate | solution.py:277
  3.4 5.3 %copy.28 = f32[6,16384]{0,1:T(8,128)} copy(f32[6,16384]{1,0:T(8,128)S(1)} %pad_maximum_fusion) | data formatting | bytes 786432 | tf_op jit(solution)/shard_map/concatenate | solution.py:277
  8.7 6.2 %gather_fusion = f32[1024,6]{1,0:T(8,128)S(1)} fusion(f32[6,16384]{0,1:T(8,128)} %copy.28, s32[1024]{0:T(1024)S(1)} %broadcast_clamp_fusion), kind=kCustom, calls=%fused_computation | custom fusion | bytes 53248 | tf_op jit(solution)/shard_map/jit(_take)/gather | solution.py:278
  14.9 0.2 copy.26
  15.2 0.7 reshape.119
  15.9 6.6 %all-to-all-start = ((f32[16,1,384]{2,1,0:T(1,128)}), f32[16,1,384]{2,1,0:T(1,128)}, u32[]{:S(2)}, u32[]{:S(2)}) async-start(f32[16,1,384]{2,1,0:T(1,128)} %reshape.119), calls=%async_computation | async-start | bytes 49152 | tf_op jit(solution)/shard_map/all_to_all | solution.py:279
  22.5 0.0 copy-done.4
  22.5 0.1 iota_compare_fusion
  22.6 0.7 lt.63
  23.3 0.0 copy-done.3
  23.3 0.7 squeeze.3
  23.9 0.0 copy-done.1
  23.9 0.2 convert_bitcast_fusion.intact_ref
  24.1 0.7 compare_select_fusion.1
  24.8 1.9 %copy.24 = bf16[27,128,128]{1,2,0:T(8,128)(2,1)S(1)} copy(bf16[27,128,128]{2,1,0:T(8,128)(2,1)} %param.17) | data formatting | bytes 1769472 | tf_op args[8]
  26.7 0.0 copy-done.2
  26.7 0.1 copy.32.hor_ref
  26.9 0.8 all-to-all-done
  27.6 0.5 broadcast.59
  28.2 1.4 %reduce = f32[16,384]{1,0:T(8,128)S(1)} reduce(f32[16,1,384]{2,1,0:T(1,128)} %all-to-all-done, f32[]{:T(128)} %broadcast.59), dimensions={1}, to_apply=%all_to_all.6.reduce_sub_computation | reduce | bytes 49156 | tf_op jit(solution)/shard_map/all_to_all | solution.py:279
  29.6 0.1 reshape.120
  29.7 0.1 reshape.112
  29.8 0.2 copy.29
  30.0 9.6 %scatter_fusion = f32[6,16384]{0,1:T(8,128)} fusion(f32[6,16384]{0,1:T(8,128)} %copy.28, s32[1024]{0:T(1024)S(1)} %bitcast.35, f32[1024,6]{1,0:T(8,128)S(1)} %copy.29), kind=kCustom, calls=%fused_computation.1 | custom fusion | bytes 77824 | tf_op jit(solution)/shard_map/scatter | solution.py:282
  39.7 12.6 %fusion = (f32[3,16384]{0,1:T(8,128)}, f32[3,16384]{0,1:T(8,128)}) fusion(f32[6,16384]{0,1:T(8,128)} %scatter_fusion), kind=kLoop, calls=%fused_computation.13 | loop fusion | bytes 786432 | tf_op jit(solution)/shard_map/slice | solution.py:291
  52.3 0.0 copy-start
  52.3 5.3 %copy.33.pos_in = f32[3,128,128]{2,1,0:T(8,128)S(1)} copy(f32[3,128,128]{0,2,1:T(8,128)} %bitcast.31) | data formatting | bytes 393216 | tf_op jit(solution)/shard_map/slice | solution.py:290
  57.5 5.2 %copy.34.vel_in = f32[3,128,128]{2,1,0:T(8,128)S(1)} copy(f32[3,128,128]{0,2,1:T(8,128)} %bitcast.30) | data formatting | bytes 393216 | tf_op jit(solution)/shard_map/slice | solution.py:291
  62.8 0.0 copy-done
  62.8 32.5 %forces.1 = (f32[3,128,128]{2,1,0:T(8,128)S(1)}, f32[3,128,128]{2,1,0:T(8,128)S(1)}) custom-call(s32[128,27]{1,0:T(8,128)S(1)} %copy.32.hor_ref, f32[27,128,128]{2,1,0:T(8,128)S(1)} %convert_bitcast_fusion.intact_ref, f32[128,128]{1,0:T(8,128)S(1)} %bitcast.29, bf16[27,128,128]{2,1,0:T(8,128)(2,1)S(1)} %bitcast.26, f32[3,128,128]{2,1,0:T(8,128)S(1)} %copy.33.pos_in, ...), custom_call_target="tpu_custom_call" | custom-call | tf_op jit(solution)/shard_map/forces/pallas_call | solution.py:238
  95.3 1.1 %copy_bitcast_fusion = (f32[3,16384]{1,0:T(4,128)}, f32[3,16384]{1,0:T(4,128)}) fusion(f32[1,3,128,128]{3,2,1,0:T(8,128)S(1)} %bitcast.28, f32[1,3,128,128]{3,2,1,0:T(8,128)S(1)} %bitcast.27), kind=kLoop, calls=%fused_computation.4 | loop fusion | bytes 786432 | tf_op jit(solution)/shard_map/reshape | solution.py:293
  (4 shorter events, 0.1 us)
Async XLA Ops:
  0.6 21.9 %copy-start.4 = (s32[1,16]{1,0:T(1,128)S(1)}, s32[1,16]{1,0:T(1,128)}, u32[]{:S(2)}) copy-start(s32[1,16]{1,0:T(1,128)} %param.13) | copy-start | bytes 196
  0.6 22.6 %copy-start.3 = (s32[1,16,64]{2,1,0:T(8,128)S(1)}, s32[1,16,64]{2,1,0:T(8,128)}, u32[]{:S(2)}) copy-start(s32[1,16,64]{2,1,0:T(8,128)} %param.12) | copy-start | bytes 12292
  0.7 23.3 %copy-start.1 = (s32[128,27,128]{2,0,1:T(8,128)S(1)}, s32[128,27,128]{2,0,1:T(8,128)}, u32[]{:S(2)}) copy-start(s32[128,27,128]{2,0,1:T(8,128)} %param.15) | copy-start | bytes 5308420
  0.7 26.1 %copy-start.2 = (s32[128,27]{0,1:T(8,128)S(1)}, s32[128,27]{0,1:T(8,128)}, u32[]{:S(2)}) copy-start(s32[128,27]{0,1:T(8,128)} %param.14) | copy-start | bytes 41476
  15.9 11.8 %all-to-all-start = ((f32[16,1,384]{2,1,0:T(1,128)}), f32[16,1,384]{2,1,0:T(1,128)}, u32[]{:S(2)}, u32[]{:S(2)}) async-start(f32[16,1,384]{2,1,0:T(1,128)} %reshape.119), calls=%async_computation | async-start | bytes 49152 | tf_op jit(solution)/shard_map/all_to_all | solution.py:279
  52.3 10.5 %copy-start = (f32[16384]{0:T(1024)S(1)}, f32[16384]{0:T(1024)}, u32[]{:S(2)}) copy-start(f32[16384]{0:T(1024)} %param.16) | copy-start | bytes 196612

commit v2 on v1

--- a/solution.py
+++ b/solution.py
@@ -9,6 +9,7 @@
 
 SUBSTEPS = 2
 LAYER = 64
+PEER_BATCH = 16
 TIME_STEP = 0.25
 MESH = pl.DeviceIdType.MESH
 F32 = jnp.float32
@@ -19,14 +20,25 @@
     blocks,
     width,
     nnz,
+    peers,
+    send_ref,
+    arrive_ref,
+    count_ref,
     hor_ref,
-    intact_ref,
+    bonds_ref,
     mod_ref,
-    wt_ref,
+    weight_ref,
     pos_in,
     vel_in,
     pos_ref,
     vel_ref,
+    out_buf,
+    in_buf,
+    spread_ref,
+    landed_ref,
+    raw_ref,
+    intact_ref,
+    wt_ref,
     onehot_ref,
     ext_ref,
     picked_ref,
@@ -37,6 +49,9 @@
     soften_ref,
     send_sem,
     recv_sem,
+    node_send_sem,
+    node_recv_sem,
+    bond_sem,
 ):
     me = lax.axis_index("wall")
     count = lax.axis_size("wall")
@@ -47,15 +62,113 @@
     left = lax.rem(me + count - 1, count)
     right = lax.rem(me + 1, count)
 
+    nodes = blocks * width
+    capacity = send_ref.shape[1]
+    shift = width.bit_length() - 1
+    batch = min(PEER_BATCH, peers)
+    lane_count = batch * capacity
+
+    bond_copies = [
+        pltpu.make_async_copy(bonds_ref.at[:, j, :], raw_ref.at[j], bond_sem.at[j]) for j in range(nnz)
+    ]
+    for copy in bond_copies:
+        copy.start()
+
     barrier = pltpu.get_barrier_semaphore()
 
-    @pl.when(has_left)
-    def _():
-        pl.semaphore_signal(barrier, inc=1, device_id={"wall": left}, device_id_type=MESH)
-
-    @pl.when(has_right)
-    def _():
-        pl.semaphore_signal(barrier, inc=1, device_id={"wall": right}, device_id_type=MESH)
+    def greet(step, carry):
+        pl.semaphore_signal(
+            barrier, inc=1, device_id={"wall": lax.rem(me + step, count)}, device_id_type=MESH
+        )
+        return carry
+
+    lax.fori_loop(1, peers, greet, 0)
+
+    def split(value):
+        high = value.astype(BF16)
+        low = (value - high.astype(F32)).astype(BF16)
+        return high, low
+
+    state = [pos_in, pos_in, pos_in, vel_in, vel_in, vel_in]
+
+    def gather_batch(step, carry):
+        rows = send_ref[pl.ds(step * batch, batch), :]
+        index = jnp.concatenate([rows[i : i + 1, :] for i in range(batch)], axis=1)
+        picked_rows = []
+        tile = 256 if lane_count % 256 == 0 else lane_count
+        splits = [jnp.concatenate(split(state[row][row % 3]), axis=1) for row in range(6)]
+        for start in range(0, lane_count, tile):
+            part = index[:, start : start + tile]
+            of_node = lax.broadcasted_iota(jnp.int32, (width, tile), 0) == (part & (width - 1))
+            of_block = lax.broadcasted_iota(jnp.int32, (blocks, tile), 0) == (part >> shift)
+            column = jnp.where(of_node, 1.0, 0.0).astype(BF16)
+            column = jnp.concatenate([column, column], axis=0)
+            values = []
+            for row in range(6):
+                found = jnp.dot(splits[row], column, preferred_element_type=F32)
+                values.append(jnp.sum(jnp.where(of_block, found, 0.0), axis=0, keepdims=True))
+            picked_rows.append(jnp.concatenate(values, axis=0))
+        picked = jnp.concatenate(picked_rows, axis=1)
+        for i in range(batch):
+            out_buf[step * batch + i, 0:6, 0:capacity] = picked[:, i * capacity : (i + 1) * capacity]
+        return carry
+
+    lax.fori_loop(0, peers // batch, gather_batch, 0)
+    in_buf[me, :, :] = jnp.zeros(in_buf.shape[1:], F32)
+    pl.semaphore_wait(barrier, peers - 1)
+
+    def node_copy(step):
+        peer = lax.rem(me + step, count)
+        return pltpu.make_async_remote_copy(
+            src_ref=out_buf.at[peer],
+            dst_ref=in_buf.at[me],
+            send_sem=node_send_sem.at[peer],
+            recv_sem=node_recv_sem.at[me],
+            device_id={"wall": peer},
+            device_id_type=MESH,
+        )
+
+    def node_arrival(step):
+        peer = lax.rem(me + step, count)
+        return pltpu.make_async_remote_copy(
+            src_ref=out_buf.at[peer],
+            dst_ref=in_buf.at[peer],
+            send_sem=node_send_sem.at[peer],
+            recv_sem=node_recv_sem.at[peer],
+            device_id={"wall": peer},
+            device_id_type=MESH,
+        )
+
+    def start_nodes(step, carry):
+        node_copy(step).start()
+        return carry
+
+    lax.fori_loop(1, peers, start_nodes, 0)
+
+    lanes = lax.broadcasted_iota(jnp.int32, (LAYER, reach), 1)
+    for half in range(2):
+        local = hor_ref[pl.ds(half * LAYER, LAYER), :] - (me * blocks - LAYER + half * LAYER)
+        for j in range(nnz):
+            hit = local[:, j : j + 1] == lanes
+            onehot_ref[half, pl.ds(j * LAYER, LAYER), :] = jnp.where(hit, 1.0, 0.0).astype(BF16)
+
+    for copy in bond_copies:
+        copy.wait()
+    stiff = jnp.zeros((blocks, width), F32)
+    zero = jnp.zeros((width, width), BF16)
+    ones = jnp.ones((16, width), BF16)
+    for j in range(nnz):
+        weight = jnp.transpose(weight_ref[j])
+        wt_ref[j] = weight
+        diag_ref[j, pl.ds(0, width), pl.ds(0, width)] = weight
+        diag_ref[j, pl.ds(width, width), pl.ds(width, width)] = weight
+        diag_ref[j, pl.ds(0, width), pl.ds(width, width)] = zero
+        diag_ref[j, pl.ds(width, width), pl.ds(0, width)] = zero
+        totals = jnp.dot(ones, weight, preferred_element_type=F32)[0:1, :]
+        intact = raw_ref[j].astype(F32)
+        intact_ref[j] = intact
+        stiff = stiff + intact * totals
+    stiff_ref[...] = stiff
 
     def halo_copy(slot, half, rows):
         wide = rows * width
@@ -98,12 +211,6 @@
     def get(slot, half, row):
         return ext_ref[slot, pl.ds(LAYER + half * LAYER, LAYER), pl.ds(row * width, width)].astype(F32)
 
-    pos_ref[...] = pos_in[...]
-    vel_ref[...] = vel_in[...]
-    for half in range(2):
-        for row in range(3):
-            put(0, half, row, pos_in[row, own(half), :].astype(BF16))
-
     @pl.when(jnp.logical_not(has_left))
     def _():
         for slot in range(slots):
@@ -114,30 +221,57 @@
         for slot in range(slots):
             ext_ref[slot, pl.ds(3 * LAYER, LAYER), :] = jnp.zeros((LAYER, 4 * width), BF16)
 
-    pl.semaphore_wait(barrier, has_left.astype(jnp.int32) + has_right.astype(jnp.int32))
-
-    send(0, 0, 3)
-    send(0, 1, 3)
-
-    lanes = lax.broadcasted_iota(jnp.int32, (LAYER, reach), 1)
-    for half in range(2):
-        local = hor_ref[own(half), :] - (me * blocks - LAYER + half * LAYER)
-        for j in range(nnz):
-            hit = local[:, j : j + 1] == lanes
-            onehot_ref[half, pl.ds(j * LAYER, LAYER), :] = jnp.where(hit, 1.0, 0.0).astype(BF16)
-
-    stiff = jnp.zeros((blocks, width), F32)
-    zero = jnp.zeros((width, width), BF16)
-    ones = jnp.ones((16, width), BF16)
-    for j in range(nnz):
-        weight = wt_ref[j]
-        diag_ref[j, pl.ds(0, width), pl.ds(0, width)] = weight
-        diag_ref[j, pl.ds(width, width), pl.ds(width, width)] = weight
-        diag_ref[j, pl.ds(0, width), pl.ds(width, width)] = zero
-        diag_ref[j, pl.ds(width, width), pl.ds(0, width)] = zero
-        totals = jnp.dot(ones, weight, preferred_element_type=F32)[0:1, :]
-        stiff = stiff + intact_ref[j] * totals
-    stiff_ref[...] = stiff
+    def finish_nodes(step, carry):
+        node_arrival(step).wait()
+        return carry
+
+    lax.fori_loop(1, peers, finish_nodes, 0)
+
+    landed_ref[...] = jnp.zeros(landed_ref.shape, F32)
+
+    def scatter_batch(step, carry):
+        rows = arrive_ref[pl.ds(step * batch, batch), :]
+        slot_ids = lax.broadcasted_iota(jnp.int32, (1, capacity), 1)
+        index = jnp.concatenate(
+            [
+                jnp.where(slot_ids < count_ref[0, step * batch + i], rows[i : i + 1, :], nodes)
+                for i in range(batch)
+            ],
+            axis=1,
+        )
+        values = jnp.concatenate(
+            [in_buf[step * batch + i][0:6, 0:capacity] for i in range(batch)], axis=1
+        )
+        high, low = split(values)
+        parts = [high.astype(F32), low.astype(F32)]
+        of_node = lax.broadcasted_iota(jnp.int32, (width, lane_count), 0) == (index & (width - 1))
+        of_block = lax.broadcasted_iota(jnp.int32, (blocks, lane_count), 0) == (index >> shift)
+        column = jnp.where(of_node, 1.0, 0.0).astype(BF16)
+        for row in range(6):
+            for k in range(2):
+                spread_ref[pl.ds((2 * row + k) * blocks, blocks), :] = jnp.where(
+                    of_block, parts[k][row : row + 1, :], 0.0
+                ).astype(BF16)
+        spread_ref[pl.ds(12 * blocks, blocks), :] = jnp.where(of_block, 1.0, 0.0).astype(BF16)
+        landed_ref[...] = landed_ref[...] + lax.dot_general(
+            spread_ref[...], column, (((1,), (1,)), ((), ())), preferred_element_type=F32
+        )
+        return carry
+
+    lax.fori_loop(0, peers // batch, scatter_batch, 0)
+
+    for half in (0, 1):
+        hit = landed_ref[pl.ds(12 * blocks + half * LAYER, LAYER), :] > 0.5
+        for row in range(6):
+            high = landed_ref[pl.ds(2 * row * blocks + half * LAYER, LAYER), :]
+            low = landed_ref[pl.ds((2 * row + 1) * blocks + half * LAYER, LAYER), :]
+            value = jnp.where(hit, high + low, state[row][row % 3, own(half), :])
+            if row < 3:
+                pos_ref[row, own(half), :] = value
+                put(0, half, row, value.astype(BF16))
+            else:
+                vel_ref[row - 3, own(half), :] = value
+        send(0, half, 3)
 
     group = 9 if nnz % 9 == 0 else nnz
 
@@ -230,35 +364,6 @@
                 halo_copy(slot, half, 3 if slot % 2 == 0 else 4).wait_send()
 
 
-def forces(horizon, intact, modulus, weight_turned, position, velocity):
-    nnz, blocks, width = intact.shape
-    slots = 2 * (SUBSTEPS + 1)
-    vmem = pl.BlockSpec(memory_space=pltpu.VMEM)
-    shape = jax.ShapeDtypeStruct((3, blocks, width), F32)
-    return pl.pallas_call(
-        functools.partial(force_kernel, blocks, width, nnz),
-        out_shape=(shape, shape),
-        in_specs=[vmem] * 6,
-        out_specs=(vmem, vmem),
-        scratch_shapes=[
-            pltpu.VMEM((2, nnz * LAYER, 3 * LAYER), BF16),
-            pltpu.VMEM((slots, 4 * LAYER, 4 * width), BF16),
-            pltpu.VMEM((nnz * LAYER, 4 * width), BF16),
-            pltpu.VMEM((nnz, 2 * width, 2 * width), BF16),
-            pltpu.VMEM((blocks, width), F32),
-            pltpu.VMEM((3, blocks, width), F32),
-            pltpu.VMEM((3, blocks, width), F32),
-            pltpu.VMEM((blocks, width), F32),
-            pltpu.SemaphoreType.DMA((slots, 2)),
-            pltpu.SemaphoreType.DMA((slots, 2)),
-        ],
-        compiler_params=pltpu.CompilerParams(
-            collective_id=0, has_side_effects=True, vmem_limit_bytes=48 * 1024 * 1024
-        ),
-        name="forces",
-    )(horizon, intact, modulus, weight_turned, position, velocity)
-
-
 def shards(
     displacement,
     velocity,
@@ -271,24 +376,55 @@
     bond_weight,
 ):
     node_count = displacement.shape[1]
-    block_count = horizon_blocks.shape[0]
-    block_width = node_count // block_count
-    capacity = send_list.shape[2]
-    stacked_state = jnp.concatenate([displacement, velocity], axis=0)
-    outgoing = jnp.take(stacked_state, send_list[0].reshape(-1), axis=1)
-    incoming = lax.all_to_all(outgoing, "wall", split_axis=1, concat_axis=1, tiled=True)
-    live_slot = jnp.arange(capacity, dtype=jnp.int32)[None, :] < recv_count[0][:, None]
-    landing = jnp.where(live_slot, arrive_list[0], node_count).reshape(-1)
-    stacked_state = stacked_state.at[:, landing].set(incoming, mode="drop")
-    blocked = stacked_state.reshape(6, block_count, block_width)
-    intact_turned = jnp.transpose(bond_intact.astype(F32), (1, 0, 2))
-    final_position, final_speed = forces(
+    blocks, nnz, width = bond_intact.shape
+    peers, capacity = send_list.shape[1:]
+    lane_count = min(PEER_BATCH, peers) * capacity
+    slots = 2 * (SUBSTEPS + 1)
+    vmem = pl.BlockSpec(memory_space=pltpu.VMEM)
+    smem = pl.BlockSpec(memory_space=pltpu.SMEM)
+    anywhere = pl.BlockSpec(memory_space=pl.ANY)
+    shape = jax.ShapeDtypeStruct((3, blocks, width), F32)
+    final_position, final_speed = pl.pallas_call(
+        functools.partial(force_kernel, blocks, width, nnz, peers),
+        out_shape=(shape, shape),
+        in_specs=[vmem, vmem, smem, vmem, anywhere, vmem, vmem, vmem, vmem],
+        out_specs=(vmem, vmem),
+        scratch_shapes=[
+            pltpu.VMEM((peers, 8, 128 * pl.cdiv(capacity, 128)), F32),
+            pltpu.VMEM((peers, 8, 128 * pl.cdiv(capacity, 128)), F32),
+            pltpu.VMEM((13 * blocks, lane_count), BF16),
+            pltpu.VMEM((13 * blocks, width), F32),
+            pltpu.VMEM((nnz, blocks, width), jnp.int32),
+            pltpu.VMEM((nnz, blocks, width), F32),
+            pltpu.VMEM((nnz, width, width), BF16),
+            pltpu.VMEM((2, nnz * LAYER, 3 * LAYER), BF16),
+            pltpu.VMEM((slots, 4 * LAYER, 4 * width), BF16),
+            pltpu.VMEM((nnz * LAYER, 4 * width), BF16),
+            pltpu.VMEM((nnz, 2 * width, 2 * width), BF16),
+            pltpu.VMEM((blocks, width), F32),
+            pltpu.VMEM((3, blocks, width), F32),
+            pltpu.VMEM((3, blocks, width), F32),
+            pltpu.VMEM((blocks, width), F32),
+            pltpu.SemaphoreType.DMA((slots, 2)),
+            pltpu.SemaphoreType.DMA((slots, 2)),
+            pltpu.SemaphoreType.DMA((peers,)),
+            pltpu.SemaphoreType.DMA((peers,)),
+            pltpu.SemaphoreType.DMA((nnz,)),
+        ],
+        compiler_params=pltpu.CompilerParams(
+            collective_id=0, has_side_effects=True, vmem_limit_bytes=52 * 1024 * 1024
+        ),
+        name="forces",
+    )(
+        send_list[0],
+        arrive_list[0],
+        recv_count,
         horizon_blocks,
-        intact_turned,
-        modulus.reshape(block_count, block_width),
-        jnp.transpose(bond_weight, (0, 2, 1)),
-        blocked[:3],
-        blocked[3:],
+        bond_intact,
+        modulus.reshape(blocks, width),
+        bond_weight,
+        displacement.reshape(3, blocks, width),
+        velocity.reshape(3, blocks, width),
     )
     return (final_position.reshape(3, node_count), final_speed.reshape(3, node_count))
 

time: 96.9 us -> 49.6 us (0.51)
  local copies, waits for them, and re-layouts: 51.4 us -> 7.53 us
  Pallas kernels: 32.5 us -> 41.2 us
  starting transfers between devices: 6.63 us -> 0 us
  other arithmetic: 4.29 us -> 0 us
    slice x3 -> x0, local copies, waits for them, and re-layouts: 23.1 us -> none  [the longest x2 17.9 us: shards(): blocked[3:]]
    scatter x1 -> x0, local copies, waits for them, and re-layouts: 9.64 us -> none  [shards(): stacked_state = stacked_state.at[:, landing].set(incoming, mode='drop')]
    pallas_call x1, Pallas kernels: 32.5 us -> 41.2 us  [shards(): pl.pallas_call(functools.partial(force_kernel, blocks, width, nnz, peers)...]
    all_to_all x1 -> x0, starting transfers between devices: 6.63 us -> none  [shards(): lax.all_to_all(outgoing, 'wall', split_axis=1, concat_axis=1, tiled=True)]
    gather x2 -> x0, local copies, waits for them, and re-layouts: 6.4 us -> none  [shards(): outgoing = jnp.take(stacked_state, send_list[0].reshape(-1), axis=1)]
    concatenate x1 -> x0, local copies, waits for them, and re-layouts: 5.29 us -> none  [shards(): stacked_state = jnp.concatenate([displacement, velocity], axis=0)]
    unnamed x14, local copies, waits for them, and re-layouts: 2.79 us -> 6.47 us
    all_to_all x1 -> x0, other arithmetic: 1.44 us -> none  [shards(): lax.all_to_all(outgoing, 'wall', split_axis=1, concat_axis=1, tiled=True)]
  transfers between devices with their start and end apart: 1 -> 0, of which waited for: 1 -> 0; matrix products, arithmetic and copies ran while one was open for 4% -> 0% of each run, Pallas kernels for 0% -> 0%
where the time goes in v2:
time: 49.6 us; the launch traced here: 49.4 us
  Pallas kernels  41.2 us (83%)
  local copies, waits for them, and re-layouts  7.53 us (15%)
  between operations  0.7 us (1%)
    pallas_call x1, Pallas kernels, shards(): pl.pallas_call(functools.partial(force_kernel, blocks, width, nnz, peers)...  41.2 us
    unnamed x14, local copies, waits for them, and re-layouts  6.47 us
    reshape x1, local copies, waits for them, and re-layouts, shards(): velocity.reshape(3, blocks, width)  1.06 us

profile of v2, /device:TPU:5, one launch (start us, length us, event | category | flops | bytes accessed | tf_op | source)
XLA Modules:
  0.0 49.4 jit_solution(17373466974913476058)
XLA Ops:
  0.6 0.8 %copy.11.hor_ref = s32[128,27]{1,0:T(8,128)S(1)} copy(s32[128,27]{0,1:T(8,128)} %param.14) | data formatting | bytes 27648 | tf_op args[5]
  1.4 1.1 %copy_bitcast_fusion.2 = (f32[3,128,128]{2,1,0:T(8,128)S(1)}, f32[3,128,128]{2,1,0:T(8,128)S(1)}) fusion(f32[1,3,128,128]{3,1,2,0:T(4,128)} %bitcast.22, f32[1,3,128,128]{3,1,2,0:T(4,128)} %bitcast.23), kind=kLoop, calls=%fused_computation.2 | loop fusion | bytes 786432 | tf_op jit(solution)/shard_map/reshape | solution.py:427
  2.5 0.0 copy-start
  2.5 0.0 copy-start.1
  2.5 0.0 copy-start.2
  2.5 0.0 copy-start.3
  2.6 0.0 copy-start.4
  2.6 3.9 %copy.12.bonds_ref = s32[128,27,128]{2,1,0:T(8,128)} copy(s32[128,27,128]{2,0,1:T(8,128)} %param.15) | data formatting | bytes 3538944 | tf_op args[6]
  6.5 0.0 copy-done
  6.5 0.0 copy-done.1
  6.5 0.0 copy-done.2
  6.5 0.0 copy-done.3
  6.5 0.0 copy-done.4
  6.5 41.2 %forces.1 = (f32[3,128,128]{2,1,0:T(8,128)S(1)}, f32[3,128,128]{2,1,0:T(8,128)S(1)}) custom-call(s32[16,64]{1,0:T(8,128)S(1)} %bitcast.20, s32[16,64]{1,0:T(8,128)S(1)} %bitcast.21, s32[1,16]{1,0:T(1,128)S(1)} %copy-done.4, s32[128,27]{1,0:T(8,128)S(1)} %copy.11.hor_ref, s32[128,27,128]{2,1,0:T(8,128)} %copy.12.bonds_ref, f32[128,128]{1,0:T(8,128)S(1)} %bitcast.19, ...), custom_call_target="tpu_custom_call" | custom-call | tf_op jit(solution)/shard_map/forces/pallas_call | solution.py:387
  47.7 0.8 %copy.21 = f32[1,3,128,128]{3,1,2,0:T(4,128)} copy(f32[1,3,128,128]{3,2,1,0:T(8,128)S(1)} %bitcast.18) | data formatting | bytes 393216
  48.6 0.8 %copy.22 = f32[1,3,128,128]{3,1,2,0:T(4,128)} copy(f32[1,3,128,128]{3,2,1,0:T(8,128)S(1)} %bitcast.17) | data formatting | bytes 393216
Async XLA Ops:
  2.5 4.0 %copy-start = (bf16[27,128,128]{2,1,0:T(8,128)(2,1)S(1)}, bf16[27,128,128]{2,1,0:T(8,128)(2,1)}, u32[]{:S(2)}) copy-start(bf16[27,128,128]{2,1,0:T(8,128)(2,1)} %weight_ref.1) | copy-start | bytes 2654212
  2.5 4.0 %copy-start.1 = (f32[16384]{0:T(1024)S(1)}, f32[16384]{0:T(1024)}, u32[]{:S(2)}) copy-start(f32[16384]{0:T(1024)} %param.16) | copy-start | bytes 196612
  2.5 4.0 %copy-start.2 = (s32[1,16,64]{2,1,0:T(8,128)S(1)}, s32[1,16,64]{2,1,0:T(8,128)}, u32[]{:S(2)}) copy-start(s32[1,16,64]{2,1,0:T(8,128)} %param.11) | copy-start | bytes 12292
  2.5 4.0 %copy-start.3 = (s32[1,16,64]{2,1,0:T(8,128)S(1)}, s32[1,16,64]{2,1,0:T(8,128)}, u32[]{:S(2)}) copy-start(s32[1,16,64]{2,1,0:T(8,128)} %param.12) | copy-start | bytes 12292
  2.6 4.0 %copy-start.4 = (s32[1,16]{1,0:T(1,128)S(1)}, s32[1,16]{1,0:T(1,128)}, u32[]{:S(2)}) copy-start(s32[1,16]{1,0:T(1,128)} %count_ref.1) | copy-start | bytes 196

commit v3 on v2

--- a/solution.py
+++ b/solution.py
@@ -1,4 +1,5 @@
 import functools
+import math
 
 import jax
 import jax.numpy as jnp
@@ -42,7 +43,6 @@
     onehot_ref,
     ext_ref,
     picked_ref,
-    diag_ref,
     stiff_ref,
     acc_ref,
     stretch_ref,
@@ -65,14 +65,11 @@
     nodes = blocks * width
     capacity = send_ref.shape[1]
     shift = width.bit_length() - 1
-    batch = min(PEER_BATCH, peers)
+    batch = math.gcd(PEER_BATCH, peers)
     lane_count = batch * capacity
 
-    bond_copies = [
-        pltpu.make_async_copy(bonds_ref.at[:, j, :], raw_ref.at[j], bond_sem.at[j]) for j in range(nnz)
-    ]
-    for copy in bond_copies:
-        copy.start()
+    bond_copy = pltpu.make_async_copy(bonds_ref, raw_ref, bond_sem)
+    bond_copy.start()
 
     barrier = pltpu.get_barrier_semaphore()
 
@@ -146,24 +143,20 @@
     lax.fori_loop(1, peers, start_nodes, 0)
 
     lanes = lax.broadcasted_iota(jnp.int32, (LAYER, reach), 1)
+    padding = jnp.zeros((-nnz % 8, blocks), jnp.int32)
+    horizon = jnp.transpose(jnp.concatenate([hor_ref[...], padding], axis=0))
     for half in range(2):
-        local = hor_ref[pl.ds(half * LAYER, LAYER), :] - (me * blocks - LAYER + half * LAYER)
+        local = horizon[half * LAYER : (half + 1) * LAYER] - (me * blocks - LAYER + half * LAYER)
         for j in range(nnz):
             hit = local[:, j : j + 1] == lanes
             onehot_ref[half, pl.ds(j * LAYER, LAYER), :] = jnp.where(hit, 1.0, 0.0).astype(BF16)
 
-    for copy in bond_copies:
-        copy.wait()
+    bond_copy.wait()
     stiff = jnp.zeros((blocks, width), F32)
-    zero = jnp.zeros((width, width), BF16)
     ones = jnp.ones((16, width), BF16)
     for j in range(nnz):
         weight = jnp.transpose(weight_ref[j])
         wt_ref[j] = weight
-        diag_ref[j, pl.ds(0, width), pl.ds(0, width)] = weight
-        diag_ref[j, pl.ds(width, width), pl.ds(width, width)] = weight
-        diag_ref[j, pl.ds(0, width), pl.ds(width, width)] = zero
-        diag_ref[j, pl.ds(width, width), pl.ds(0, width)] = zero
         totals = jnp.dot(ones, weight, preferred_element_type=F32)[0:1, :]
         intact = raw_ref[j].astype(F32)
         intact_ref[j] = intact
@@ -287,20 +280,12 @@
         for j in range(nnz):
             part = pl.ds(j * LAYER, LAYER)
             mask = intact_ref[j, own(half), :]
-            weight = diag_ref[j]
-            for pair in range(2):
-                first = 2 * pair
-                if first + 1 < rows:
-                    product = jnp.dot(
-                        picked_ref[part, pl.ds(first * width, 2 * width)], weight, preferred_element_type=F32
-                    )
-                    sums[first] = sums[first] + product[:, :width] * mask
-                    sums[first + 1] = sums[first + 1] + product[:, width:] * mask
-                else:
-                    product = jnp.dot(
-                        picked_ref[part, pl.ds(first * width, width)], wt_ref[j], preferred_element_type=F32
-                    )
-                    sums[first] = sums[first] + product * mask
+            stacked = jnp.concatenate(
+                [picked_ref[part, pl.ds(row * width, width)] for row in range(rows)], axis=0
+            )
+            product = jnp.dot(stacked, wt_ref[j], preferred_element_type=F32)
+            for row in range(rows):
+                sums[row] = sums[row] + product[row * LAYER : (row + 1) * LAYER] * mask
         return sums
 
     def evaluation(t, carry):
@@ -378,7 +363,7 @@
     node_count = displacement.shape[1]
     blocks, nnz, width = bond_intact.shape
     peers, capacity = send_list.shape[1:]
-    lane_count = min(PEER_BATCH, peers) * capacity
+    lane_count = math.gcd(PEER_BATCH, peers) * capacity
     slots = 2 * (SUBSTEPS + 1)
     vmem = pl.BlockSpec(memory_space=pltpu.VMEM)
     smem = pl.BlockSpec(memory_space=pltpu.SMEM)
@@ -400,7 +385,6 @@
             pltpu.VMEM((2, nnz * LAYER, 3 * LAYER), BF16),
             pltpu.VMEM((slots, 4 * LAYER, 4 * width), BF16),
             pltpu.VMEM((nnz * LAYER, 4 * width), BF16),
-            pltpu.VMEM((nnz, 2 * width, 2 * width), BF16),
             pltpu.VMEM((blocks, width), F32),
             pltpu.VMEM((3, blocks, width), F32),
             pltpu.VMEM((3, blocks, width), F32),
@@ -409,7 +393,7 @@
             pltpu.SemaphoreType.DMA((slots, 2)),
             pltpu.SemaphoreType.DMA((peers,)),
             pltpu.SemaphoreType.DMA((peers,)),
-            pltpu.SemaphoreType.DMA((nnz,)),
+            pltpu.SemaphoreType.DMA,
         ],
         compiler_params=pltpu.CompilerParams(
             collective_id=0, has_side_effects=True, vmem_limit_bytes=52 * 1024 * 1024
@@ -419,8 +403,8 @@
         send_list[0],
         arrive_list[0],
         recv_count,
-        horizon_blocks,
-        bond_intact,
+        jnp.transpose(horizon_blocks),
+        jnp.transpose(bond_intact, (1, 0, 2)),
         modulus.reshape(blocks, width),
         bond_weight,
         displacement.reshape(3, blocks, width),

time: 49.6 us -> 45.3 us (0.913)
  Pallas kernels: 41.2 us -> 36.8 us
    pallas_call x1, Pallas kernels: 41.2 us -> 36.8 us  [shards(): pl.pallas_call(functools.partial(force_kernel, blocks, width, nnz, peers)...]
where the time goes in v3:
time: 45.3 us; the launch traced here: 44.9 us
  Pallas kernels  36.8 us (81%)
  local copies, waits for them, and re-layouts  7.5 us (17%)
  between operations  0.66 us (1%)
    pallas_call x1, Pallas kernels, shards(): pl.pallas_call(functools.partial(force_kernel, blocks, width, nnz, peers)...  36.8 us
    unnamed x14, local copies, waits for them, and re-layouts  6.44 us
    reshape x1, local copies, waits for them, and re-layouts, shards(): velocity.reshape(3, blocks, width)  1.06 us

profile of v3, /device:TPU:5, one launch (start us, length us, event | category | flops | bytes accessed | tf_op | source)
XLA Modules:
  0.0 44.9 jit_solution(15049272803124882513)
XLA Ops:
  0.6 1.1 %copy_bitcast_fusion.2 = (f32[3,128,128]{2,1,0:T(8,128)S(1)}, f32[3,128,128]{2,1,0:T(8,128)S(1)}) fusion(f32[1,3,128,128]{3,1,2,0:T(4,128)} %bitcast.26, f32[1,3,128,128]{3,1,2,0:T(4,128)} %bitcast.27), kind=kLoop, calls=%fused_computation.2 | loop fusion | bytes 786432 | tf_op jit(solution)/shard_map/reshape | solution.py:411
  1.7 0.0 copy-start
  1.7 1.2 %copy-done = bf16[27,128,128]{2,1,0:T(8,128)(2,1)S(1)} copy-done((bf16[27,128,128]{2,1,0:T(8,128)(2,1)S(1)}, bf16[27,128,128]{2,1,0:T(8,128)(2,1)}, u32[]{:S(2)}) %copy-start) | copy-done | bytes 884760
  2.9 0.0 copy-start.1
  2.9 0.8 %copy-done.1 = f32[16384]{0:T(1024)S(1)} copy-done((f32[16384]{0:T(1024)S(1)}, f32[16384]{0:T(1024)}, u32[]{:S(2)}) %copy-start.1) | copy-done | bytes 65560
  3.7 0.0 copy-start.2
  3.7 0.7 %copy-done.2 = s32[128,27]{0,1:T(8,128)S(1)} copy-done((s32[128,27]{0,1:T(8,128)S(1)}, s32[128,27]{0,1:T(8,128)}, u32[]{:S(2)}) %copy-start.2) | copy-done | bytes 13848
  4.4 0.0 copy-start.3
  4.4 0.7 %copy-done.3 = s32[1,16,64]{2,1,0:T(8,128)S(1)} copy-done((s32[1,16,64]{2,1,0:T(8,128)S(1)}, s32[1,16,64]{2,1,0:T(8,128)}, u32[]{:S(2)}) %copy-start.3) | copy-done | bytes 4120
  5.1 0.0 copy-start.4
  5.1 0.7 %copy-done.4 = s32[1,16,64]{2,1,0:T(8,128)S(1)} copy-done((s32[1,16,64]{2,1,0:T(8,128)S(1)}, s32[1,16,64]{2,1,0:T(8,128)}, u32[]{:S(2)}) %copy-start.4) | copy-done | bytes 4120
  5.8 0.0 copy-start.5
  5.8 0.7 %copy-done.5 = s32[1,16]{1,0:T(1,128)S(1)} copy-done((s32[1,16]{1,0:T(1,128)S(1)}, s32[1,16]{1,0:T(1,128)}, u32[]{:S(2)}) %copy-start.5) | copy-done | bytes 88
  6.5 36.8 %forces.1 = (f32[3,128,128]{2,1,0:T(8,128)S(1)}, f32[3,128,128]{2,1,0:T(8,128)S(1)}) custom-call(s32[16,64]{1,0:T(8,128)S(1)} %bitcast.23, s32[16,64]{1,0:T(8,128)S(1)} %bitcast.24, s32[1,16]{1,0:T(1,128)S(1)} %copy-done.5, s32[27,128]{1,0:T(8,128)S(1)} %bitcast.22, s32[27,128,128]{2,1,0:T(8,128)} %bitcast.25, f32[128,128]{1,0:T(8,128)S(1)} %bitcast.21, ...), custom_call_target="tpu_custom_call" | custom-call | tf_op jit(solution)/shard_map/forces/pallas_call | solution.py:372
  43.3 0.8 %copy.19 = f32[1,3,128,128]{3,1,2,0:T(4,128)} copy(f32[1,3,128,128]{3,2,1,0:T(8,128)S(1)} %bitcast.20) | data formatting | bytes 393216
  44.1 0.8 %copy.20 = f32[1,3,128,128]{3,1,2,0:T(4,128)} copy(f32[1,3,128,128]{3,2,1,0:T(8,128)S(1)} %bitcast.19) | data formatting | bytes 393216
Async XLA Ops:
  1.7 1.2 %copy-start = (bf16[27,128,128]{2,1,0:T(8,128)(2,1)S(1)}, bf16[27,128,128]{2,1,0:T(8,128)(2,1)}, u32[]{:S(2)}) copy-start(bf16[27,128,128]{2,1,0:T(8,128)(2,1)} %weight_ref.1) | copy-start | bytes 2654212
  2.9 0.8 %copy-start.1 = (f32[16384]{0:T(1024)S(1)}, f32[16384]{0:T(1024)}, u32[]{:S(2)}) copy-start(f32[16384]{0:T(1024)} %param.16) | copy-start | bytes 196612
  3.7 0.7 %copy-start.2 = (s32[128,27]{0,1:T(8,128)S(1)}, s32[128,27]{0,1:T(8,128)}, u32[]{:S(2)}) copy-start(s32[128,27]{0,1:T(8,128)} %param.14) | copy-start | bytes 41476
  4.4 0.7 %copy-start.3 = (s32[1,16,64]{2,1,0:T(8,128)S(1)}, s32[1,16,64]{2,1,0:T(8,128)}, u32[]{:S(2)}) copy-start(s32[1,16,64]{2,1,0:T(8,128)} %param.11) | copy-start | bytes 12292
  5.1 0.7 %copy-start.4 = (s32[1,16,64]{2,1,0:T(8,128)S(1)}, s32[1,16,64]{2,1,0:T(8,128)}, u32[]{:S(2)}) copy-start(s32[1,16,64]{2,1,0:T(8,128)} %param.12) | copy-start | bytes 12292
  5.8 0.7 %copy-start.5 = (s32[1,16]{1,0:T(1,128)S(1)}, s32[1,16]{1,0:T(1,128)}, u32[]{:S(2)}) copy-start(s32[1,16]{1,0:T(1,128)} %count_ref.1) | copy-start | bytes 196

commit v4 on v3

--- a/solution.py
+++ b/solution.py
@@ -22,17 +22,27 @@
     width,
     nnz,
     peers,
+    send_hbm,
+    arrive_hbm,
+    count_hbm,
+    hor_hbm,
+    bonds_hbm,
+    mod_hbm,
+    weight_hbm,
+    pos_hbm,
+    vel_hbm,
+    pos_ref,
+    vel_ref,
     send_ref,
     arrive_ref,
     count_ref,
     hor_ref,
-    bonds_ref,
     mod_ref,
     weight_ref,
+    pos_raw,
+    vel_raw,
     pos_in,
     vel_in,
-    pos_ref,
-    vel_ref,
     out_buf,
     in_buf,
     spread_ref,
@@ -51,7 +61,7 @@
     recv_sem,
     node_send_sem,
     node_recv_sem,
-    bond_sem,
+    fetch_sem,
 ):
     me = lax.axis_index("wall")
     count = lax.axis_size("wall")
@@ -68,8 +78,14 @@
     batch = math.gcd(PEER_BATCH, peers)
     lane_count = batch * capacity
 
-    bond_copy = pltpu.make_async_copy(bonds_ref, raw_ref, bond_sem)
-    bond_copy.start()
+    pairs = [(send_hbm.at[0], send_ref)]
+    pairs += [(pos_hbm, pos_raw), (vel_hbm, vel_raw)]
+    early = len(pairs)
+    pairs += [(hor_hbm, hor_ref), (weight_hbm, weight_ref), (bonds_hbm, raw_ref)]
+    pairs += [(arrive_hbm.at[0], arrive_ref), (count_hbm, count_ref), (mod_hbm, mod_ref)]
+    fetches = [pltpu.make_async_copy(pair[0], pair[1], fetch_sem.at[i]) for i, pair in enumerate(pairs)]
+    for fetch in fetches:
+        fetch.start()
 
     barrier = pltpu.get_barrier_semaphore()
 
@@ -86,6 +102,11 @@
         low = (value - high.astype(F32)).astype(BF16)
         return high, low
 
+    for fetch in fetches[:early]:
+        fetch.wait()
+    for row in range(3):
+        pos_in[row] = pos_raw[:, row, :]
+        vel_in[row] = vel_raw[:, row, :]
     state = [pos_in, pos_in, pos_in, vel_in, vel_in, vel_in]
 
     def gather_batch(step, carry):
@@ -143,6 +164,7 @@
     lax.fori_loop(1, peers, start_nodes, 0)
 
     lanes = lax.broadcasted_iota(jnp.int32, (LAYER, reach), 1)
+    fetches[early].wait()
     padding = jnp.zeros((-nnz % 8, blocks), jnp.int32)
     horizon = jnp.transpose(jnp.concatenate([hor_ref[...], padding], axis=0))
     for half in range(2):
@@ -151,7 +173,8 @@
             hit = local[:, j : j + 1] == lanes
             onehot_ref[half, pl.ds(j * LAYER, LAYER), :] = jnp.where(hit, 1.0, 0.0).astype(BF16)
 
-    bond_copy.wait()
+    for fetch in fetches[early + 1 :]:
+        fetch.wait()
     stiff = jnp.zeros((blocks, width), F32)
     ones = jnp.ones((16, width), BF16)
     for j in range(nnz):
@@ -366,15 +389,24 @@
     lane_count = math.gcd(PEER_BATCH, peers) * capacity
     slots = 2 * (SUBSTEPS + 1)
     vmem = pl.BlockSpec(memory_space=pltpu.VMEM)
-    smem = pl.BlockSpec(memory_space=pltpu.SMEM)
-    anywhere = pl.BlockSpec(memory_space=pl.ANY)
+    hbm = pl.BlockSpec(memory_space=pltpu.HBM)
     shape = jax.ShapeDtypeStruct((3, blocks, width), F32)
     final_position, final_speed = pl.pallas_call(
         functools.partial(force_kernel, blocks, width, nnz, peers),
         out_shape=(shape, shape),
-        in_specs=[vmem, vmem, smem, vmem, anywhere, vmem, vmem, vmem, vmem],
+        in_specs=[hbm] * 9,
         out_specs=(vmem, vmem),
         scratch_shapes=[
+            pltpu.VMEM((peers, capacity), jnp.int32),
+            pltpu.VMEM((peers, capacity), jnp.int32),
+            pltpu.SMEM((1, peers), jnp.int32),
+            pltpu.VMEM((nnz, blocks), jnp.int32),
+            pltpu.VMEM((blocks, width), F32),
+            pltpu.VMEM((nnz, width, width), BF16),
+            pltpu.VMEM((blocks, 3, width), F32),
+            pltpu.VMEM((blocks, 3, width), F32),
+            pltpu.VMEM((3, blocks, width), F32),
+            pltpu.VMEM((3, blocks, width), F32),
             pltpu.VMEM((peers, 8, 128 * pl.cdiv(capacity, 128)), F32),
             pltpu.VMEM((peers, 8, 128 * pl.cdiv(capacity, 128)), F32),
             pltpu.VMEM((13 * blocks, lane_count), BF16),
@@ -393,22 +425,22 @@
             pltpu.SemaphoreType.DMA((slots, 2)),
             pltpu.SemaphoreType.DMA((peers,)),
             pltpu.SemaphoreType.DMA((peers,)),
-            pltpu.SemaphoreType.DMA,
+            pltpu.SemaphoreType.DMA((9,)),
         ],
         compiler_params=pltpu.CompilerParams(
-            collective_id=0, has_side_effects=True, vmem_limit_bytes=52 * 1024 * 1024
+            collective_id=0, has_side_effects=True, vmem_limit_bytes=67043328
         ),
         name="forces",
     )(
-        send_list[0],
-        arrive_list[0],
+        send_list,
+        arrive_list,
         recv_count,
         jnp.transpose(horizon_blocks),
         jnp.transpose(bond_intact, (1, 0, 2)),
         modulus.reshape(blocks, width),
         bond_weight,
-        displacement.reshape(3, blocks, width),
-        velocity.reshape(3, blocks, width),
+        jnp.transpose(displacement.reshape(3, blocks, width), (1, 0, 2)),
+        jnp.transpose(velocity.reshape(3, blocks, width), (1, 0, 2)),
     )
     return (final_position.reshape(3, node_count), final_speed.reshape(3, node_count))
 

time: 45.3 us -> 40 us (0.88)
  local copies, waits for them, and re-layouts: 7.5 us -> 2.08 us
    unnamed x14 -> x0, local copies, waits for them, and re-layouts: 6.44 us -> none
    reshape x1, local copies, waits for them, and re-layouts: 1.06 us -> 2.08 us  [shards(): final_speed.reshape(3, node_count)]
where the time goes in v4:
time: 40 us; the launch traced here: 39.8 us
  Pallas kernels  37 us (92%)
  local copies, waits for them, and re-layouts  2.08 us (5%)
  between operations  0.64 us (2%)
    pallas_call x1, Pallas kernels, shards(): pl.pallas_call(functools.partial(force_kernel, blocks, width, nnz, peers)...  37 us
    reshape x1, local copies, waits for them, and re-layouts, shards(): final_speed.reshape(3, node_count)  2.08 us

profile of v4, /device:TPU:5, one launch (start us, length us, event | category | flops | bytes accessed | tf_op | source)
XLA Modules:
  0.0 39.8 jit_solution(17990479511045602062)
XLA Ops:
  0.6 37.0 %forces.1 = (f32[3,128,128]{2,1,0:T(8,128)}, f32[3,128,128]{2,1,0:T(8,128)}) custom-call(s32[1,16,64]{2,1,0:T(8,128)} %send_hbm.1, s32[1,16,64]{2,1,0:T(8,128)} %arrive_hbm.1, s32[1,16]{1,0:T(1,128)} %count_hbm.1, s32[27,128]{1,0:T(8,128)} %bitcast.21, s32[27,128,128]{2,1,0:T(8,128)} %bitcast.15, f32[128,128]{1,0:T(8,128)} %bitcast.20, ...), custom_call_target="tpu_custom_call" | custom-call | tf_op jit(solution)/shard_map/forces/pallas_call | solution.py:394
  37.7 2.1 %copy_bitcast_fusion = (f32[3,16384]{1,0:T(4,128)}, f32[3,16384]{1,0:T(4,128)}) fusion(f32[1,3,128,128]{3,2,1,0:T(8,128)} %bitcast.19, f32[1,3,128,128]{3,2,1,0:T(8,128)} %bitcast.18), kind=kLoop, calls=%fused_computation | loop fusion | bytes 786432 | tf_op jit(solution)/shard_map/reshape | solution.py:445
